TPU v7x, 256 devices: a whole 4x4x8 slice. The times are simulated.
256 devices in a mesh: sec: 4 (over y), ty: 32 (over z, x), tx: 2 (over core).
Axes of the slice: x: 4, y: 4, z: 8, core: 2. Of those that a mesh axis runs over, the one named last changes fastest.
Arguments:
- images: float32 [4, 2048, 1024], P('sec', 'ty', 'tx'), may hold values from -6 to 6
- tissue_rows: int32 [32], replicated, may hold values from 21 to 64, as said below
Outputs:
- aligned_flow: float32 [2, 4, 2048, 1024], P(None, 'sec', 'ty', 'tx')
Inputs may be any that keep to these rules, and one draw needn't show every extreme that they name: `tissue_rows`: tissue row counts grow along the rows of tiles, about threefold from the first to the last.
All inputs are finite; a program needn't handle non-finite values.
Results may differ from a plain program's by a relative error of at most 0.00002.
Values sent between devices are 32-bit elements; how exact they have to be, the bound alone decides.
A program may use at most 64 MiB of HBM per device.

v0:
```python
import jax
import jax.numpy as jnp
from jax import lax
from jax.sharding import PartitionSpec as P

SWEEPS = 12
RELAX = 4
RESTRICT = 4


alpha_term = 0.5
stack_weight = 1.0
mesh_weight = 0.5
relax_total = 5.0


def passed_along(block, axis, distance):
    devices = range(lax.axis_size(axis))
    route = [(i - distance, i) for i in devices if i - distance in devices]
    return lax.ppermute(block, axis, route)


def padded_2(x, sides, width):
    for axis, dim in sides:
        size, length = (lax.axis_size(axis), x.shape[dim])
        up = [(i, (i + 1) % size) for i in range(size - 1)]
        down = [(j, i) for i, j in up]
        last = lax.slice_in_dim(x, length - width, length, axis=dim)
        leading = lax.slice_in_dim(x, 0, width, axis=dim)
        before = lax.ppermute(last, axis, up)
        after = lax.ppermute(leading, axis, down)
        x = jnp.concatenate([before, x, after], axis=dim)
    return x


def sweep_once(flow, grad_x, grad_y, grad_t, denom, mask):
    padded = jnp.pad(flow, ((0, 0), (0, 0), (1, 1), (1, 1)))
    mean = 0.25 * (
        padded[:, :, :-2, 1:-1]
        + padded[:, :, 2:, 1:-1]
        + (padded[:, :, 1:-1, :-2] + padded[:, :, 1:-1, 2:])
    )
    share = (grad_x * mean[0] + grad_y * mean[1] + grad_t) / denom
    return jnp.stack([mean[0] - grad_x * share, mean[1] - grad_y * share]) * mask


def relax_step(padded, coarse):
    stack_sum = padded[:, :-2, 1:-1, 1:-1] + padded[:, 2:, 1:-1, 1:-1]
    mesh_sum = (
        padded[:, 1:-1, :-2, 1:-1]
        + padded[:, 1:-1, 2:, 1:-1]
        + (padded[:, 1:-1, 1:-1, :-2] + padded[:, 1:-1, 1:-1, 2:])
    )
    return (coarse + stack_weight * stack_sum + mesh_weight * mesh_sum) / relax_total


def shards(images, tissue_rows):
    sec_dev, rows, cols = images.shape
    n_sec = lax.axis_size("sec")
    n_ty = lax.axis_size("ty")
    n_tx = lax.axis_size("tx")
    after = passed_along(images[0], "sec", -1)
    after = jnp.where(lax.axis_index("sec") == n_sec - 1, images[-1], after)
    frames = jnp.concatenate([images, after[None]], 0)
    depth = 1
    wide = padded_2(frames, (("ty", 1), ("tx", 2)), 2)
    grad_x = 0.25 * (
        wide[:-1, 1:-1, 2:] - wide[:-1, 1:-1, :-2] + (wide[1:, 1:-1, 2:] - wide[1:, 1:-1, :-2])
    )
    grad_y = 0.25 * (
        wide[:-1, 2:, 1:-1] - wide[:-1, :-2, 1:-1] + (wide[1:, 2:, 1:-1] - wide[1:, :-2, 1:-1])
    )
    grad_t = wide[1:, 1:-1, 1:-1] - wide[:-1, 1:-1, 1:-1]
    denom = alpha_term + grad_x * grad_x + grad_y * grad_y
    row_ids = lax.axis_index("ty") * rows - depth + jnp.arange(rows + 2 * depth, dtype=jnp.int32)
    col_ids = lax.axis_index("tx") * cols - depth + jnp.arange(cols + 2 * depth, dtype=jnp.int32)
    row_inside = (row_ids >= 0) & (row_ids < n_ty * rows)
    tile = jnp.clip(row_ids, 0, n_ty * rows - 1) // rows
    local = row_ids - tile * rows
    limit = jnp.sum(
        jnp.where(
            tile[:, None] == jnp.arange(n_ty, dtype=jnp.int32)[None, :], tissue_rows[None, :], 0
        ),
        axis=1,
    )
    row_mask = row_inside & ((local + limit // 2) % rows < limit)
    col_mask = (col_ids >= 0) & (col_ids < n_tx * cols)
    mask = (row_mask[:, None] & col_mask[None, :]).astype(jnp.float32)
    flow = jnp.zeros((2, sec_dev, rows, cols), jnp.float32)
    for group in range(SWEEPS // depth):
        margin = padded_2(flow, (("ty", 2), ("tx", 3)), 1)
        margin = sweep_once(margin, grad_x, grad_y, grad_t, denom, mask)
        flow = margin[:, :, depth : depth + rows, depth : depth + cols]
    own_mask = mask[depth : depth + rows, depth : depth + cols]
    coarse_rows = rows // RESTRICT
    coarse_cols = cols // RESTRICT
    coarse = flow.reshape(2, sec_dev, coarse_rows, RESTRICT, coarse_cols, RESTRICT).mean(
        axis=(3, 5)
    )
    disp = coarse
    for sweep in range(RELAX):
        padded = padded_2(disp, (("sec", 1), ("ty", 2), ("tx", 3)), 1)
        disp = relax_step(padded, coarse)
    back = jnp.repeat(jnp.repeat(disp, RESTRICT, axis=2), RESTRICT, axis=3)
    return flow + own_mask * back


def solution(mesh):
    placed = (P("sec", "ty", "tx"), P())
    return jax.shard_map(
        shards, mesh=mesh, in_specs=placed, out_specs=P(None, "sec", "ty", "tx"), check_vma=False
    )
```

profile of v0, /device:TPU:127, one launch (start us, length us, event | category | flops | bytes accessed | tf_op | source)
XLA Modules:
  0.0 465.8 jit_solution(15662051386116737553)
XLA Ops:
  2.5 6.1 %collective-permute-start = (f32[2,1,1,512]{2,3,1,0:T(8,128)S(1)}, f32[2,1,1,512]{2,3,1,0:T(8,128)S(1)}, u32[]{:S(2)}, u32[]{:S(2)}) collective-permute-start(f32[2,1,1,512]{2,3,1,0:T(8,128)S(1)} %broadcast.335), channel_id=1, source_target_pairs={{0,2},{2,4},{4,6},{6,8},{8,10},{10,12},{12,14},{14,16},{16,18},{18... | collective-permute-start | bytes 12296 | tf_op jit(solution)/shard_map/ppermute | solution.py:30
  13.0 5.0 %collective-permute-done.1 = f32[2,1,1,512]{2,3,1,0:T(8,128)S(1)} collective-permute-done((f32[2,1,1,512]{2,3,1,0:T(8,128)S(1)}, f32[2,1,1,512]{2,3,1,0:T(8,128)S(1)}, u32[]{:S(2)}, u32[]{:S(2)}) %collective-permute-start.1) | collective-permute-done | bytes 4128 | tf_op jit(solution)/shard_map/ppermute | solution.py:31
  24.4 7.4 %collective-permute-start.5 = (f32[2,2,512]{1,2,0:T(8,128)S(1)}, f32[2,2,512]{1,2,0:T(8,128)S(1)}, u32[]{:S(2)}, u32[]{:S(2)}) collective-permute-start(f32[2,2,512]{1,2,0:T(8,128)S(1)} %get-tuple-element.81), channel_id=1, source_target_pairs={{0,2},{2,4},{4,6},{6,8},{8,10},{10,12},{12,14},{14,16},{16,18},{18... | collective-permute-start | bytes 24584 | tf_op jit(solution)/shard_map/ppermute | solution.py:30
  34.2 9.2 %collective-permute-done.5 = f32[2,2,512]{1,2,0:T(8,128)S(1)} collective-permute-done((f32[2,2,512]{1,2,0:T(8,128)S(1)}, f32[2,2,512]{1,2,0:T(8,128)S(1)}, u32[]{:S(2)}, u32[]{:S(2)}) %collective-permute-start.5) | collective-permute-done | bytes 8224 | tf_op jit(solution)/shard_map/ppermute | solution.py:30
  43.4 7.4 %collective-permute-done.6 = f32[2,2,512]{1,2,0:T(8,128)S(1)} collective-permute-done((f32[2,2,512]{1,2,0:T(8,128)S(1)}, f32[2,2,512]{1,2,0:T(8,128)S(1)}, u32[]{:S(2)}, u32[]{:S(2)}) %collective-permute-start.6) | collective-permute-done | bytes 8224 | tf_op jit(solution)/shard_map/ppermute | solution.py:31
  63.7 9.5 %collective-permute-done.9 = f32[2,1,1,512]{2,3,1,0:T(8,128)S(1)} collective-permute-done((f32[2,1,1,512]{2,3,1,0:T(8,128)S(1)}, f32[2,1,1,512]{2,3,1,0:T(8,128)S(1)}, u32[]{:S(2)}, u32[]{:S(2)}) %collective-permute-start.9) | collective-permute-done | bytes 4128 | tf_op jit(solution)/shard_map/ppermute | solution.py:30
  73.2 5.2 %collective-permute-done.10 = f32[2,1,1,512]{2,3,1,0:T(8,128)S(1)} collective-permute-done((f32[2,1,1,512]{2,3,1,0:T(8,128)S(1)}, f32[2,1,1,512]{2,3,1,0:T(8,128)S(1)}, u32[]{:S(2)}, u32[]{:S(2)}) %collective-permute-start.10) | collective-permute-done | bytes 4128 | tf_op jit(solution)/shard_map/ppermute | solution.py:31
  90.8 9.5 %collective-permute-done.13 = f32[2,1,1,512]{2,3,1,0:T(8,128)S(1)} collective-permute-done((f32[2,1,1,512]{2,3,1,0:T(8,128)S(1)}, f32[2,1,1,512]{2,3,1,0:T(8,128)S(1)}, u32[]{:S(2)}, u32[]{:S(2)}) %collective-permute-start.13) | collective-permute-done | bytes 4128 | tf_op jit(solution)/shard_map/ppermute | solution.py:30
  100.3 5.2 %collective-permute-done.14 = f32[2,1,1,512]{2,3,1,0:T(8,128)S(1)} collective-permute-done((f32[2,1,1,512]{2,3,1,0:T(8,128)S(1)}, f32[2,1,1,512]{2,3,1,0:T(8,128)S(1)}, u32[]{:S(2)}, u32[]{:S(2)}) %collective-permute-start.14) | collective-permute-done | bytes 4128 | tf_op jit(solution)/shard_map/ppermute | solution.py:31
  117.9 9.5 %collective-permute-done.17 = f32[2,1,1,512]{2,3,1,0:T(8,128)S(1)} collective-permute-done((f32[2,1,1,512]{2,3,1,0:T(8,128)S(1)}, f32[2,1,1,512]{2,3,1,0:T(8,128)S(1)}, u32[]{:S(2)}, u32[]{:S(2)}) %collective-permute-start.17) | collective-permute-done | bytes 4128 | tf_op jit(solution)/shard_map/ppermute | solution.py:30
  127.5 5.2 %collective-permute-done.18 = f32[2,1,1,512]{2,3,1,0:T(8,128)S(1)} collective-permute-done((f32[2,1,1,512]{2,3,1,0:T(8,128)S(1)}, f32[2,1,1,512]{2,3,1,0:T(8,128)S(1)}, u32[]{:S(2)}, u32[]{:S(2)}) %collective-permute-start.18) | collective-permute-done | bytes 4128 | tf_op jit(solution)/shard_map/ppermute | solution.py:31
  145.0 9.5 %collective-permute-done.21 = f32[2,1,1,512]{2,3,1,0:T(8,128)S(1)} collective-permute-done((f32[2,1,1,512]{2,3,1,0:T(8,128)S(1)}, f32[2,1,1,512]{2,3,1,0:T(8,128)S(1)}, u32[]{:S(2)}, u32[]{:S(2)}) %collective-permute-start.21) | collective-permute-done | bytes 4128 | tf_op jit(solution)/shard_map/ppermute | solution.py:30
  154.6 5.2 %collective-permute-done.22 = f32[2,1,1,512]{2,3,1,0:T(8,128)S(1)} collective-permute-done((f32[2,1,1,512]{2,3,1,0:T(8,128)S(1)}, f32[2,1,1,512]{2,3,1,0:T(8,128)S(1)}, u32[]{:S(2)}, u32[]{:S(2)}) %collective-permute-start.22) | collective-permute-done | bytes 4128 | tf_op jit(solution)/shard_map/ppermute | solution.py:31
  172.2 9.5 %collective-permute-done.25 = f32[2,1,1,512]{2,3,1,0:T(8,128)S(1)} collective-permute-done((f32[2,1,1,512]{2,3,1,0:T(8,128)S(1)}, f32[2,1,1,512]{2,3,1,0:T(8,128)S(1)}, u32[]{:S(2)}, u32[]{:S(2)}) %collective-permute-start.25) | collective-permute-done | bytes 4128 | tf_op jit(solution)/shard_map/ppermute | solution.py:30
  181.7 5.2 %collective-permute-done.26 = f32[2,1,1,512]{2,3,1,0:T(8,128)S(1)} collective-permute-done((f32[2,1,1,512]{2,3,1,0:T(8,128)S(1)}, f32[2,1,1,512]{2,3,1,0:T(8,128)S(1)}, u32[]{:S(2)}, u32[]{:S(2)}) %collective-permute-start.26) | collective-permute-done | bytes 4128 | tf_op jit(solution)/shard_map/ppermute | solution.py:31
  199.3 9.5 %collective-permute-done.29 = f32[2,1,1,512]{2,3,1,0:T(8,128)S(1)} collective-permute-done((f32[2,1,1,512]{2,3,1,0:T(8,128)S(1)}, f32[2,1,1,512]{2,3,1,0:T(8,128)S(1)}, u32[]{:S(2)}, u32[]{:S(2)}) %collective-permute-start.29) | collective-permute-done | bytes 4128 | tf_op jit(solution)/shard_map/ppermute | solution.py:30
  208.8 5.2 %collective-permute-done.30 = f32[2,1,1,512]{2,3,1,0:T(8,128)S(1)} collective-permute-done((f32[2,1,1,512]{2,3,1,0:T(8,128)S(1)}, f32[2,1,1,512]{2,3,1,0:T(8,128)S(1)}, u32[]{:S(2)}, u32[]{:S(2)}) %collective-permute-start.30) | collective-permute-done | bytes 4128 | tf_op jit(solution)/shard_map/ppermute | solution.py:31
  226.4 9.5 %collective-permute-done.33 = f32[2,1,1,512]{2,3,1,0:T(8,128)S(1)} collective-permute-done((f32[2,1,1,512]{2,3,1,0:T(8,128)S(1)}, f32[2,1,1,512]{2,3,1,0:T(8,128)S(1)}, u32[]{:S(2)}, u32[]{:S(2)}) %collective-permute-start.33) | collective-permute-done | bytes 4128 | tf_op jit(solution)/shard_map/ppermute | solution.py:30
  235.9 5.2 %collective-permute-done.34 = f32[2,1,1,512]{2,3,1,0:T(8,128)S(1)} collective-permute-done((f32[2,1,1,512]{2,3,1,0:T(8,128)S(1)}, f32[2,1,1,512]{2,3,1,0:T(8,128)S(1)}, u32[]{:S(2)}, u32[]{:S(2)}) %collective-permute-start.34) | collective-permute-done | bytes 4128 | tf_op jit(solution)/shard_map/ppermute | solution.py:31
  253.5 9.5 %collective-permute-done.37 = f32[2,1,1,512]{2,3,1,0:T(8,128)S(1)} collective-permute-done((f32[2,1,1,512]{2,3,1,0:T(8,128)S(1)}, f32[2,1,1,512]{2,3,1,0:T(8,128)S(1)}, u32[]{:S(2)}, u32[]{:S(2)}) %collective-permute-start.37) | collective-permute-done | bytes 4128 | tf_op jit(solution)/shard_map/ppermute | solution.py:30
  263.0 5.2 %collective-permute-done.38 = f32[2,1,1,512]{2,3,1,0:T(8,128)S(1)} collective-permute-done((f32[2,1,1,512]{2,3,1,0:T(8,128)S(1)}, f32[2,1,1,512]{2,3,1,0:T(8,128)S(1)}, u32[]{:S(2)}, u32[]{:S(2)}) %collective-permute-start.38) | collective-permute-done | bytes 4128 | tf_op jit(solution)/shard_map/ppermute | solution.py:31
  280.6 9.5 %collective-permute-done.41 = f32[2,1,1,512]{2,3,1,0:T(8,128)S(1)} collective-permute-done((f32[2,1,1,512]{2,3,1,0:T(8,128)S(1)}, f32[2,1,1,512]{2,3,1,0:T(8,128)S(1)}, u32[]{:S(2)}, u32[]{:S(2)}) %collective-permute-start.41) | collective-permute-done | bytes 4128 | tf_op jit(solution)/shard_map/ppermute | solution.py:30
  290.2 5.2 %collective-permute-done.42 = f32[2,1,1,512]{2,3,1,0:T(8,128)S(1)} collective-permute-done((f32[2,1,1,512]{2,3,1,0:T(8,128)S(1)}, f32[2,1,1,512]{2,3,1,0:T(8,128)S(1)}, u32[]{:S(2)}, u32[]{:S(2)}) %collective-permute-start.42) | collective-permute-done | bytes 4128 | tf_op jit(solution)/shard_map/ppermute | solution.py:31
  307.8 9.5 %collective-permute-done.45 = f32[2,1,1,512]{2,3,1,0:T(8,128)S(1)} collective-permute-done((f32[2,1,1,512]{2,3,1,0:T(8,128)S(1)}, f32[2,1,1,512]{2,3,1,0:T(8,128)S(1)}, u32[]{:S(2)}, u32[]{:S(2)}) %collective-permute-start.45) | collective-permute-done | bytes 4128 | tf_op jit(solution)/shard_map/ppermute | solution.py:30
  317.3 5.2 %collective-permute-done.46 = f32[2,1,1,512]{2,3,1,0:T(8,128)S(1)} collective-permute-done((f32[2,1,1,512]{2,3,1,0:T(8,128)S(1)}, f32[2,1,1,512]{2,3,1,0:T(8,128)S(1)}, u32[]{:S(2)}, u32[]{:S(2)}) %collective-permute-start.46) | collective-permute-done | bytes 4128 | tf_op jit(solution)/shard_map/ppermute | solution.py:31
  334.9 9.5 %collective-permute-done.49 = f32[2,1,1,512]{2,3,0,1:T(8,128)S(1)} collective-permute-done((f32[2,1,1,512]{2,3,0,1:T(8,128)S(1)}, f32[2,1,1,512]{2,3,0,1:T(8,128)S(1)}, u32[]{:S(2)}, u32[]{:S(2)}) %collective-permute-start.49) | collective-permute-done | bytes 4128 | tf_op jit(solution)/shard_map/ppermute | solution.py:30
  344.4 5.2 %collective-permute-done.50 = f32[2,1,1,512]{2,3,0,1:T(8,128)S(1)} collective-permute-done((f32[2,1,1,512]{2,3,0,1:T(8,128)S(1)}, f32[2,1,1,512]{2,3,0,1:T(8,128)S(1)}, u32[]{:S(2)}, u32[]{:S(2)}) %collective-permute-start.50) | collective-permute-done | bytes 4128 | tf_op jit(solution)/shard_map/ppermute | solution.py:31
  357.0 10.1 %reshape.566 = f32[2,16,4,128,4]{4,3,2,1,0:T(8,128)} reshape(f32[2,1,64,512]{3,2,0,1:T(8,128)S(1)} %copy.56) | data formatting | bytes 524288 | tf_op jit(solution)/shard_map/reshape | solution.py:97
  388.9 4.8 %collective-permute-start.58 = (f32[2,3,18,1]{3,2,0,1:T(8,128)S(1)}, f32[2,3,18,1]{3,2,0,1:T(8,128)S(1)}, u32[]{:S(2)}, u32[]{:S(2)}) collective-permute-start(f32[2,3,18,1]{3,2,0,1:T(8,128)S(1)} %get-tuple-element.90), channel_id=1, source_target_pairs={{1,0},{3,2},{5,4},{7,6},{9,8},{11,10},{13,12},{15,14},{17,16},{19,... | collective-permute-start | bytes 1304 | tf_op jit(solution)/shard_map/ppermute | solution.py:31
  412.3 4.8 %collective-permute-start.64 = (f32[2,3,18,1]{3,2,0,1:T(8,128)S(1)}, f32[2,3,18,1]{3,2,0,1:T(8,128)S(1)}, u32[]{:S(2)}, u32[]{:S(2)}) collective-permute-start(f32[2,3,18,1]{3,2,0,1:T(8,128)S(1)} %get-tuple-element.88), channel_id=1, source_target_pairs={{1,0},{3,2},{5,4},{7,6},{9,8},{11,10},{13,12},{15,14},{17,16},{19,... | collective-permute-start | bytes 1304 | tf_op jit(solution)/shard_map/ppermute | solution.py:31
  435.7 4.8 %collective-permute-start.70 = (f32[2,3,18,1]{3,2,0,1:T(8,128)S(1)}, f32[2,3,18,1]{3,2,0,1:T(8,128)S(1)}, u32[]{:S(2)}, u32[]{:S(2)}) collective-permute-start(f32[2,3,18,1]{3,2,0,1:T(8,128)S(1)} %get-tuple-element.86), channel_id=1, source_target_pairs={{1,0},{3,2},{5,4},{7,6},{9,8},{11,10},{13,12},{15,14},{17,16},{19,... | collective-permute-start | bytes 1304 | tf_op jit(solution)/shard_map/ppermute | solution.py:31
  458.6 4.8 %collective-permute-start.76 = (f32[2,3,18,1]{3,2,0,1:T(8,128)S(1)}, f32[2,3,18,1]{3,2,0,1:T(8,128)S(1)}, u32[]{:S(2)}, u32[]{:S(2)}) collective-permute-start(f32[2,3,18,1]{3,2,0,1:T(8,128)S(1)} %get-tuple-element.84), channel_id=1, source_target_pairs={{1,0},{3,2},{5,4},{7,6},{9,8},{11,10},{13,12},{15,14},{17,16},{19,... | collective-permute-start | bytes 1304 | tf_op jit(solution)/shard_map/ppermute | solution.py:31
  (246 shorter events, 237.4 us)
Async XLA Ops:
  0.0 18.0 %collective-permute-start.1 = (f32[2,1,1,512]{2,3,1,0:T(8,128)S(1)}, f32[2,1,1,512]{2,3,1,0:T(8,128)S(1)}, u32[]{:S(2)}, u32[]{:S(2)}) collective-permute-start(f32[2,1,1,512]{2,3,1,0:T(8,128)S(1)} %broadcast.335), channel_id=1, source_target_pairs={{2,0},{4,2},{6,4},{8,6},{10,8},{12,10},{14,12},{16,14},{18,16},{20... | collective-permute-start | bytes 12296 | tf_op jit(solution)/shard_map/ppermute | solution.py:31
  2.5 16.5 %collective-permute-start = (f32[2,1,1,512]{2,3,1,0:T(8,128)S(1)}, f32[2,1,1,512]{2,3,1,0:T(8,128)S(1)}, u32[]{:S(2)}, u32[]{:S(2)}) collective-permute-start(f32[2,1,1,512]{2,3,1,0:T(8,128)S(1)} %broadcast.335), channel_id=1, source_target_pairs={{0,2},{2,4},{4,6},{6,8},{8,10},{10,12},{12,14},{14,16},{16,18},{18... | collective-permute-start | bytes 12296 | tf_op jit(solution)/shard_map/ppermute | solution.py:30
  9.7 14.4 %collective-permute-start.4 = (f32[64,512]{0,1:T(8,128)S(1)}, f32[64,512]{0,1:T(8,128)S(1)}, u32[]{:S(2)}, u32[]{:S(2)}) collective-permute-start(f32[64,512]{0,1:T(8,128)S(1)} %bitcast.331), channel_id=1, source_target_pairs={{64,0},{128,64},{192,128},{65,1},{129,65},{193,129},{66,2},{130,66... | collective-permute-start | bytes 393224 | tf_op jit(solution)/shard_map/ppermute | solution.py:20
  19.1 14.6 %collective-permute-start.2 = (f32[2,1,66,1]{2,3,1,0:T(1,128)S(1)}, f32[2,1,66,1]{2,3,1,0:T(1,128)S(1)}, u32[]{:S(2)}, u32[]{:S(2)}) collective-permute-start(f32[2,1,66,1]{2,3,1,0:T(1,128)S(1)} %get-tuple-element.37), channel_id=1, source_target_pairs={{0,1},{2,3},{4,5},{6,7},{8,9},{10,11},{12,13},{14,15},{16,17},{18,... | collective-permute-start | bytes 1592 | tf_op jit(solution)/shard_map/ppermute | solution.py:30
  20.4 13.4 %collective-permute-start.3 = (f32[2,1,66,1]{2,3,1,0:T(1,128)S(1)}, f32[2,1,66,1]{2,3,1,0:T(1,128)S(1)}, u32[]{:S(2)}, u32[]{:S(2)}) collective-permute-start(f32[2,1,66,1]{2,3,1,0:T(1,128)S(1)} %get-tuple-element.38), channel_id=1, source_target_pairs={{1,0},{3,2},{5,4},{7,6},{9,8},{11,10},{13,12},{15,14},{17,16},{19,... | collective-permute-start | bytes 1592 | tf_op jit(solution)/shard_map/ppermute | solution.py:31
  24.4 19.0 %collective-permute-start.5 = (f32[2,2,512]{1,2,0:T(8,128)S(1)}, f32[2,2,512]{1,2,0:T(8,128)S(1)}, u32[]{:S(2)}, u32[]{:S(2)}) collective-permute-start(f32[2,2,512]{1,2,0:T(8,128)S(1)} %get-tuple-element.81), channel_id=1, source_target_pairs={{0,2},{2,4},{4,6},{6,8},{8,10},{10,12},{12,14},{14,16},{16,18},{18... | collective-permute-start | bytes 24584 | tf_op jit(solution)/shard_map/ppermute | solution.py:30
  31.8 19.0 %collective-permute-start.6 = (f32[2,2,512]{1,2,0:T(8,128)S(1)}, f32[2,2,512]{1,2,0:T(8,128)S(1)}, u32[]{:S(2)}, u32[]{:S(2)}) collective-permute-start(f32[2,2,512]{1,2,0:T(8,128)S(1)} %get-tuple-element.82), channel_id=1, source_target_pairs={{2,0},{4,2},{6,4},{8,6},{10,8},{12,10},{14,12},{16,14},{18,16},{20... | collective-permute-start | bytes 24584 | tf_op jit(solution)/shard_map/ppermute | solution.py:31
  58.2 15.0 %collective-permute-start.9 = (f32[2,1,1,512]{2,3,1,0:T(8,128)S(1)}, f32[2,1,1,512]{2,3,1,0:T(8,128)S(1)}, u32[]{:S(2)}, u32[]{:S(2)}) collective-permute-start(f32[2,1,1,512]{2,3,1,0:T(8,128)S(1)} %get-tuple-element.79), channel_id=1, source_target_pairs={{0,2},{2,4},{4,6},{6,8},{8,10},{10,12},{12,14},{14,16},{16,18},{18... | collective-permute-start | bytes 12296 | tf_op jit(solution)/shard_map/ppermute | solution.py:30
  60.1 18.4 %collective-permute-start.10 = (f32[2,1,1,512]{2,3,1,0:T(8,128)S(1)}, f32[2,1,1,512]{2,3,1,0:T(8,128)S(1)}, u32[]{:S(2)}, u32[]{:S(2)}) collective-permute-start(f32[2,1,1,512]{2,3,1,0:T(8,128)S(1)} %get-tuple-element.80), channel_id=1, source_target_pairs={{2,0},{4,2},{6,4},{8,6},{10,8},{12,10},{14,12},{16,14},{18,16},{20... | collective-permute-start | bytes 12296 | tf_op jit(solution)/shard_map/ppermute | solution.py:31
  85.3 15.0 %collective-permute-start.13 = (f32[2,1,1,512]{2,3,1,0:T(8,128)S(1)}, f32[2,1,1,512]{2,3,1,0:T(8,128)S(1)}, u32[]{:S(2)}, u32[]{:S(2)}) collective-permute-start(f32[2,1,1,512]{2,3,1,0:T(8,128)S(1)} %get-tuple-element.77), channel_id=1, source_target_pairs={{0,2},{2,4},{4,6},{6,8},{8,10},{10,12},{12,14},{14,16},{16,18},{18... | collective-permute-start | bytes 12296 | tf_op jit(solution)/shard_map/ppermute | solution.py:30
  87.2 18.4 %collective-permute-start.14 = (f32[2,1,1,512]{2,3,1,0:T(8,128)S(1)}, f32[2,1,1,512]{2,3,1,0:T(8,128)S(1)}, u32[]{:S(2)}, u32[]{:S(2)}) collective-permute-start(f32[2,1,1,512]{2,3,1,0:T(8,128)S(1)} %get-tuple-element.78), channel_id=1, source_target_pairs={{2,0},{4,2},{6,4},{8,6},{10,8},{12,10},{14,12},{16,14},{18,16},{20... | collective-permute-start | bytes 12296 | tf_op jit(solution)/shard_map/ppermute | solution.py:31
  112.4 15.0 %collective-permute-start.17 = (f32[2,1,1,512]{2,3,1,0:T(8,128)S(1)}, f32[2,1,1,512]{2,3,1,0:T(8,128)S(1)}, u32[]{:S(2)}, u32[]{:S(2)}) collective-permute-start(f32[2,1,1,512]{2,3,1,0:T(8,128)S(1)} %get-tuple-element.75), channel_id=1, source_target_pairs={{0,2},{2,4},{4,6},{6,8},{8,10},{10,12},{12,14},{14,16},{16,18},{18... | collective-permute-start | bytes 12296 | tf_op jit(solution)/shard_map/ppermute | solution.py:30
  114.3 18.4 %collective-permute-start.18 = (f32[2,1,1,512]{2,3,1,0:T(8,128)S(1)}, f32[2,1,1,512]{2,3,1,0:T(8,128)S(1)}, u32[]{:S(2)}, u32[]{:S(2)}) collective-permute-start(f32[2,1,1,512]{2,3,1,0:T(8,128)S(1)} %get-tuple-element.76), channel_id=1, source_target_pairs={{2,0},{4,2},{6,4},{8,6},{10,8},{12,10},{14,12},{16,14},{18,16},{20... | collective-permute-start | bytes 12296 | tf_op jit(solution)/shard_map/ppermute | solution.py:31
  139.5 15.0 %collective-permute-start.21 = (f32[2,1,1,512]{2,3,1,0:T(8,128)S(1)}, f32[2,1,1,512]{2,3,1,0:T(8,128)S(1)}, u32[]{:S(2)}, u32[]{:S(2)}) collective-permute-start(f32[2,1,1,512]{2,3,1,0:T(8,128)S(1)} %get-tuple-element.73), channel_id=1, source_target_pairs={{0,2},{2,4},{4,6},{6,8},{8,10},{10,12},{12,14},{14,16},{16,18},{18... | collective-permute-start | bytes 12296 | tf_op jit(solution)/shard_map/ppermute | solution.py:30
  141.5 18.4 %collective-permute-start.22 = (f32[2,1,1,512]{2,3,1,0:T(8,128)S(1)}, f32[2,1,1,512]{2,3,1,0:T(8,128)S(1)}, u32[]{:S(2)}, u32[]{:S(2)}) collective-permute-start(f32[2,1,1,512]{2,3,1,0:T(8,128)S(1)} %get-tuple-element.74), channel_id=1, source_target_pairs={{2,0},{4,2},{6,4},{8,6},{10,8},{12,10},{14,12},{16,14},{18,16},{20... | collective-permute-start | bytes 12296 | tf_op jit(solution)/shard_map/ppermute | solution.py:31
  166.7 15.0 %collective-permute-start.25 = (f32[2,1,1,512]{2,3,1,0:T(8,128)S(1)}, f32[2,1,1,512]{2,3,1,0:T(8,128)S(1)}, u32[]{:S(2)}, u32[]{:S(2)}) collective-permute-start(f32[2,1,1,512]{2,3,1,0:T(8,128)S(1)} %get-tuple-element.71), channel_id=1, source_target_pairs={{0,2},{2,4},{4,6},{6,8},{8,10},{10,12},{12,14},{14,16},{16,18},{18... | collective-permute-start | bytes 12296 | tf_op jit(solution)/shard_map/ppermute | solution.py:30
  168.6 18.4 %collective-permute-start.26 = (f32[2,1,1,512]{2,3,1,0:T(8,128)S(1)}, f32[2,1,1,512]{2,3,1,0:T(8,128)S(1)}, u32[]{:S(2)}, u32[]{:S(2)}) collective-permute-start(f32[2,1,1,512]{2,3,1,0:T(8,128)S(1)} %get-tuple-element.72), channel_id=1, source_target_pairs={{2,0},{4,2},{6,4},{8,6},{10,8},{12,10},{14,12},{16,14},{18,16},{20... | collective-permute-start | bytes 12296 | tf_op jit(solution)/shard_map/ppermute | solution.py:31
  193.8 15.0 %collective-permute-start.29 = (f32[2,1,1,512]{2,3,1,0:T(8,128)S(1)}, f32[2,1,1,512]{2,3,1,0:T(8,128)S(1)}, u32[]{:S(2)}, u32[]{:S(2)}) collective-permute-start(f32[2,1,1,512]{2,3,1,0:T(8,128)S(1)} %get-tuple-element.69), channel_id=1, source_target_pairs={{0,2},{2,4},{4,6},{6,8},{8,10},{10,12},{12,14},{14,16},{16,18},{18... | collective-permute-start | bytes 12296 | tf_op jit(solution)/shard_map/ppermute | solution.py:30
  195.7 18.4 %collective-permute-start.30 = (f32[2,1,1,512]{2,3,1,0:T(8,128)S(1)}, f32[2,1,1,512]{2,3,1,0:T(8,128)S(1)}, u32[]{:S(2)}, u32[]{:S(2)}) collective-permute-start(f32[2,1,1,512]{2,3,1,0:T(8,128)S(1)} %get-tuple-element.70), channel_id=1, source_target_pairs={{2,0},{4,2},{6,4},{8,6},{10,8},{12,10},{14,12},{16,14},{18,16},{20... | collective-permute-start | bytes 12296 | tf_op jit(solution)/shard_map/ppermute | solution.py:31
  220.9 15.0 %collective-permute-start.33 = (f32[2,1,1,512]{2,3,1,0:T(8,128)S(1)}, f32[2,1,1,512]{2,3,1,0:T(8,128)S(1)}, u32[]{:S(2)}, u32[]{:S(2)}) collective-permute-start(f32[2,1,1,512]{2,3,1,0:T(8,128)S(1)} %get-tuple-element.67), channel_id=1, source_target_pairs={{0,2},{2,4},{4,6},{6,8},{8,10},{10,12},{12,14},{14,16},{16,18},{18... | collective-permute-start | bytes 12296 | tf_op jit(solution)/shard_map/ppermute | solution.py:30
  222.8 18.4 %collective-permute-start.34 = (f32[2,1,1,512]{2,3,1,0:T(8,128)S(1)}, f32[2,1,1,512]{2,3,1,0:T(8,128)S(1)}, u32[]{:S(2)}, u32[]{:S(2)}) collective-permute-start(f32[2,1,1,512]{2,3,1,0:T(8,128)S(1)} %get-tuple-element.68), channel_id=1, source_target_pairs={{2,0},{4,2},{6,4},{8,6},{10,8},{12,10},{14,12},{16,14},{18,16},{20... | collective-permute-start | bytes 12296 | tf_op jit(solution)/shard_map/ppermute | solution.py:31
  248.0 15.0 %collective-permute-start.37 = (f32[2,1,1,512]{2,3,1,0:T(8,128)S(1)}, f32[2,1,1,512]{2,3,1,0:T(8,128)S(1)}, u32[]{:S(2)}, u32[]{:S(2)}) collective-permute-start(f32[2,1,1,512]{2,3,1,0:T(8,128)S(1)} %get-tuple-element.65), channel_id=1, source_target_pairs={{0,2},{2,4},{4,6},{6,8},{8,10},{10,12},{12,14},{14,16},{16,18},{18... | collective-permute-start | bytes 12296 | tf_op jit(solution)/shard_map/ppermute | solution.py:30
  249.9 18.4 %collective-permute-start.38 = (f32[2,1,1,512]{2,3,1,0:T(8,128)S(1)}, f32[2,1,1,512]{2,3,1,0:T(8,128)S(1)}, u32[]{:S(2)}, u32[]{:S(2)}) collective-permute-start(f32[2,1,1,512]{2,3,1,0:T(8,128)S(1)} %get-tuple-element.66), channel_id=1, source_target_pairs={{2,0},{4,2},{6,4},{8,6},{10,8},{12,10},{14,12},{16,14},{18,16},{20... | collective-permute-start | bytes 12296 | tf_op jit(solution)/shard_map/ppermute | solution.py:31
  275.1 15.0 %collective-permute-start.41 = (f32[2,1,1,512]{2,3,1,0:T(8,128)S(1)}, f32[2,1,1,512]{2,3,1,0:T(8,128)S(1)}, u32[]{:S(2)}, u32[]{:S(2)}) collective-permute-start(f32[2,1,1,512]{2,3,1,0:T(8,128)S(1)} %get-tuple-element.63), channel_id=1, source_target_pairs={{0,2},{2,4},{4,6},{6,8},{8,10},{10,12},{12,14},{14,16},{16,18},{18... | collective-permute-start | bytes 12296 | tf_op jit(solution)/shard_map/ppermute | solution.py:30
  277.1 18.4 %collective-permute-start.42 = (f32[2,1,1,512]{2,3,1,0:T(8,128)S(1)}, f32[2,1,1,512]{2,3,1,0:T(8,128)S(1)}, u32[]{:S(2)}, u32[]{:S(2)}) collective-permute-start(f32[2,1,1,512]{2,3,1,0:T(8,128)S(1)} %get-tuple-element.64), channel_id=1, source_target_pairs={{2,0},{4,2},{6,4},{8,6},{10,8},{12,10},{14,12},{16,14},{18,16},{20... | collective-permute-start | bytes 12296 | tf_op jit(solution)/shard_map/ppermute | solution.py:31
  302.3 15.0 %collective-permute-start.45 = (f32[2,1,1,512]{2,3,1,0:T(8,128)S(1)}, f32[2,1,1,512]{2,3,1,0:T(8,128)S(1)}, u32[]{:S(2)}, u32[]{:S(2)}) collective-permute-start(f32[2,1,1,512]{2,3,1,0:T(8,128)S(1)} %get-tuple-element.61), channel_id=1, source_target_pairs={{0,2},{2,4},{4,6},{6,8},{8,10},{10,12},{12,14},{14,16},{16,18},{18... | collective-permute-start | bytes 12296 | tf_op jit(solution)/shard_map/ppermute | solution.py:30
  304.2 18.4 %collective-permute-start.46 = (f32[2,1,1,512]{2,3,1,0:T(8,128)S(1)}, f32[2,1,1,512]{2,3,1,0:T(8,128)S(1)}, u32[]{:S(2)}, u32[]{:S(2)}) collective-permute-start(f32[2,1,1,512]{2,3,1,0:T(8,128)S(1)} %get-tuple-element.62), channel_id=1, source_target_pairs={{2,0},{4,2},{6,4},{8,6},{10,8},{12,10},{14,12},{16,14},{18,16},{20... | collective-permute-start | bytes 12296 | tf_op jit(solution)/shard_map/ppermute | solution.py:31
  329.4 15.0 %collective-permute-start.49 = (f32[2,1,1,512]{2,3,0,1:T(8,128)S(1)}, f32[2,1,1,512]{2,3,0,1:T(8,128)S(1)}, u32[]{:S(2)}, u32[]{:S(2)}) collective-permute-start(f32[2,1,1,512]{2,3,0,1:T(8,128)S(1)} %get-tuple-element.59), channel_id=1, source_target_pairs={{0,2},{2,4},{4,6},{6,8},{8,10},{10,12},{12,14},{14,16},{16,18},{18... | collective-permute-start | bytes 12296 | tf_op jit(solution)/shard_map/ppermute | solution.py:30
  331.3 18.4 %collective-permute-start.50 = (f32[2,1,1,512]{2,3,0,1:T(8,128)S(1)}, f32[2,1,1,512]{2,3,0,1:T(8,128)S(1)}, u32[]{:S(2)}, u32[]{:S(2)}) collective-permute-start(f32[2,1,1,512]{2,3,0,1:T(8,128)S(1)} %get-tuple-element.60), channel_id=1, source_target_pairs={{2,0},{4,2},{6,4},{8,6},{10,8},{12,10},{14,12},{16,14},{18,16},{20... | collective-permute-start | bytes 12296 | tf_op jit(solution)/shard_map/ppermute | solution.py:31
  379.9 7.7 %collective-permute-start.56 = (f32[2,3,1,128]{3,2,0,1:T(1,128)S(1)}, f32[2,3,1,128]{3,2,0,1:T(1,128)S(1)}, u32[]{:S(2)}, u32[]{:S(2)}) collective-permute-start(f32[2,3,1,128]{3,2,0,1:T(1,128)S(1)} %get-tuple-element.98), channel_id=1, source_target_pairs={{2,0},{4,2},{6,4},{8,6},{10,8},{12,10},{14,12},{16,14},{18,16},{20... | collective-permute-start | bytes 9224 | tf_op jit(solution)/shard_map/ppermute | solution.py:31
  403.2 7.7 %collective-permute-start.62 = (f32[2,3,1,128]{3,2,0,1:T(1,128)S(1)}, f32[2,3,1,128]{3,2,0,1:T(1,128)S(1)}, u32[]{:S(2)}, u32[]{:S(2)}) collective-permute-start(f32[2,3,1,128]{3,2,0,1:T(1,128)S(1)} %get-tuple-element.96), channel_id=1, source_target_pairs={{2,0},{4,2},{6,4},{8,6},{10,8},{12,10},{14,12},{16,14},{18,16},{20... | collective-permute-start | bytes 9224 | tf_op jit(solution)/shard_map/ppermute | solution.py:31
  426.6 7.7 %collective-permute-start.68 = (f32[2,3,1,128]{3,2,0,1:T(1,128)S(1)}, f32[2,3,1,128]{3,2,0,1:T(1,128)S(1)}, u32[]{:S(2)}, u32[]{:S(2)}) collective-permute-start(f32[2,3,1,128]{3,2,0,1:T(1,128)S(1)} %get-tuple-element.94), channel_id=1, source_target_pairs={{2,0},{4,2},{6,4},{8,6},{10,8},{12,10},{14,12},{16,14},{18,16},{20... | collective-permute-start | bytes 9224 | tf_op jit(solution)/shard_map/ppermute | solution.py:31
  (45 other events, 208.4 us)
where the time goes:
time: 468 us; the launch traced here: 466 us
  waiting for transfers between devices  227 us (49%)
  starting transfers between devices  195 us (42%)
  other arithmetic  23.5 us (5%)
  local copies, waits for them, and re-layouts  18.8 us (4%)
    ppermute x38, waiting for transfers between devices, padded_2(): before = lax.ppermute(last, axis, up)  128 us
    ppermute x38, starting transfers between devices, padded_2(): after = lax.ppermute(leading, axis, down)  124 us
    ppermute x38, waiting for transfers between devices, padded_2(): after = lax.ppermute(leading, axis, down)  99.3 us
    ppermute x38, starting transfers between devices, padded_2(): before = lax.ppermute(last, axis, up)  69.3 us
    reshape x1, local copies, waits for them, and re-layouts, shards(): flow.reshape(2, sec_dev, coarse_rows, RESTRICT, coarse_cols, RESTRICT)  10.1 us
  transfers between devices with their start and end apart: 77, of which 50 were waited for; matrix products, arithmetic and copies ran while one was open for 1% of the time, Pallas kernels for 0%

commit v1 on v0

v1 whole, which is shorter than its diff:
```python
import functools

import jax
import jax.numpy as jnp
import numpy as np
from jax import lax
from jax.experimental import pallas as pl
from jax.experimental.pallas import tpu as pltpu
from jax.sharding import PartitionSpec as P

MESH = pl.DeviceIdType.MESH
F32 = jnp.float32
BF16 = jnp.bfloat16

SWEEPS = 12
RELAX = 4
ALPHA = 0.5
STACK = 1.0
COUPLE = 0.5
TOTAL = 5.0

N_SEC = 4
ROWS = 64
COLS = 512
HALO = 32
EXT = ROWS + 2 * HALO
NM = EXT // 8
TILES = 5
STEP = 104


def section_table():
    w = {(0, 0): 1.0}
    for _ in range(RELAX):
        new = {(0, 0): 1.0}
        for (a, b), value in w.items():
            new[(a + 1, b)] = new.get((a + 1, b), 0.0) + value
            new[(a, b + 1)] = new.get((a, b + 1), 0.0) + value
        w = {key: value / TOTAL for key, value in new.items()}
    path = np.zeros((N_SEC, N_SEC))
    for i in range(N_SEC - 1):
        path[i, i + 1] = path[i + 1, i] = STACK
    table = np.zeros((N_SEC, N_SEC, RELAX + 1))
    for (a, b), value in w.items():
        power = np.linalg.matrix_power(path, a)
        for src in range(N_SEC):
            for shift in range(N_SEC):
                table[src, shift, b] += value * power[(src + shift) % N_SEC, src] * COUPLE**b
    return table.astype(np.float32).reshape(-1)


def split3(x):
    hi = x.astype(BF16)
    rest = x - hi.astype(F32)
    mid = rest.astype(BF16)
    low = (rest - mid.astype(F32)).astype(BF16)
    return jnp.concatenate([hi, mid, low], axis=0)


def dot3(x, w):
    n = x.shape[0]
    y = jnp.dot(split3(x), w, preferred_element_type=F32)
    return y[:n] + y[n : 2 * n] + y[2 * n :]


def kernel(
    tissue_ref, table_ref, img_ref, out_ref,
    own, nxt, coef, flow, pooled, pool_w, up_w, sent, got, packed, outbuf,
    load_sem, send_sem, recv_sem, csend_sem, crecv_sem, out_sem,
):
    n_ty = lax.axis_size("ty")
    sec = lax.axis_index("sec")
    ty = lax.axis_index("ty")
    tx = lax.axis_index("tx")
    before = {"ty": lax.rem(ty + n_ty - 1, n_ty)}
    after = {"ty": lax.rem(ty + 1, n_ty)}
    partner = {"tx": 1 - tx}
    others = [{"sec": lax.rem(sec + d, N_SEC)} for d in range(1, N_SEC)]

    loads = [
        pltpu.make_async_copy(
            img_ref.at[0, :, pl.ds(128 * j, 128)], own.at[j, pl.ds(HALO, ROWS), :], load_sem.at[j]
        )
        for j in range(4)
    ]
    for load in loads:
        load.start()

    barrier = pltpu.get_barrier_semaphore()
    peers = [before, after, partner] + others
    for peer in peers:
        pl.semaphore_signal(barrier, inc=1, device_id=peer, device_id_type=MESH)

    lane = lax.broadcasted_iota(jnp.int32, (8, 128), 1)
    sub = lax.broadcasted_iota(jnp.int32, (8, 128), 0)

    def start_of(j):
        return jnp.where(tx == 0, STEP * j - 1, 385 - STEP * j)

    n_id = lax.broadcasted_iota(jnp.int32, (128, 256), 1)
    k_id = lax.broadcasted_iota(jnp.int32, (128, 256), 0)
    q_of = jnp.where(n_id < 128, n_id - 8, n_id - 24)
    for j in range(TILES):
        col = k_id + start_of(j)
        lo, hi = (12, 115)
        if j == 0:
            lo = jnp.where(tx == 0, 1, 12)
            hi = jnp.where(tx == 0, 115, 126)
        hit = (k_id >= lo) & (k_id <= hi) & (lax.shift_right_arithmetic(col, 2) == q_of)
        pool_w[pl.ds(128 * j, 128), :] = jnp.where(hit, 0.0625, 0.0).astype(BF16)
    un = lax.broadcasted_iota(jnp.int32, (128, 128), 1)
    uq = lax.broadcasted_iota(jnp.int32, (128, 128), 0)
    for i in range(4):
        a = jnp.where(tx == 0, i, 3 - i)
        hit = lax.shift_right_arithmetic(un + 128 * a, 2) == uq
        up_w[:, pl.ds(128 * i, 128)] = jnp.where(hit, 1.0, 0.0).astype(BF16)

    for load in loads:
        load.wait()
    pl.semaphore_wait(barrier, len(peers))

    edge = jnp.where(tx == 0, 3, 0)
    top, mid, low = (pl.ds(HALO, HALO), pl.ds(HALO, ROWS), pl.ds(ROWS, HALO))
    head, tail = (pl.ds(0, HALO), pl.ds(HALO + ROWS, HALO))
    four = pl.ds(0, 4)

    def send(k, src, dst, device):
        copy = pltpu.make_async_remote_copy(
            src_ref=src, dst_ref=dst, send_sem=send_sem.at[k], recv_sem=recv_sem.at[k],
            device_id=device, device_id_type=MESH,
        )
        copy.start()
        return copy

    previous = {"sec": lax.rem(sec + N_SEC - 1, N_SEC)}
    c0 = send(0, own.at[four, top], nxt.at[four, top], previous)
    c1 = send(1, own.at[four, low], nxt.at[four, low], previous)
    c2 = send(2, own.at[four, top], own.at[four, tail], before)
    c3 = send(3, own.at[four, low], own.at[four, head], after)
    c4 = send(4, own.at[edge, mid], own.at[4, mid], partner)
    c0.wait_recv()
    c5 = send(5, nxt.at[four, top], nxt.at[four, tail], before)
    c6 = send(6, nxt.at[edge, top], nxt.at[4, top], partner)
    c1.wait_recv()
    c7 = send(7, nxt.at[four, low], nxt.at[four, head], after)
    c8 = send(8, nxt.at[edge, low], nxt.at[4, low], partner)
    c2.wait_recv()
    c9 = send(9, own.at[edge, tail], own.at[4, tail], partner)
    c3.wait_recv()
    c10 = send(10, own.at[edge, head], own.at[4, head], partner)
    c5.wait_recv()
    c11 = send(11, nxt.at[edge, tail], nxt.at[4, tail], partner)
    c7.wait_recv()
    c12 = send(12, nxt.at[edge, head], nxt.at[4, head], partner)
    copies = [c0, c1, c2, c3, c4, c5, c6, c7, c8, c9, c10, c11, c12]

    k_own = tissue_ref[ty]
    k_before = jnp.where(ty > 0, tissue_ref[lax.rem(ty + n_ty - 1, n_ty)], 0)
    k_after = jnp.where(ty < n_ty - 1, tissue_ref[lax.rem(ty + 1, n_ty)], 0)
    limit = jnp.where(sub < 2, k_before, jnp.where(sub < 6, k_own, k_after))
    row0 = NM * sub + (ROWS * ty - HALO)

    def tile_body(j, carry):
        @pl.when(j == 4)
        def _():
            for c in (c4, c6, c8, c9, c10, c11, c12):
                c.wait_recv()

        start = start_of(j)
        pos = lax.rem(start + 640, 640)
        ta = pos // 128
        tb = lax.rem(ta + 1, TILES)
        off = pos - 128 * ta
        ta = jnp.where((j == 0) & (ta == 4), 0, ta)
        tb = jnp.where((j == 0) & (tb == 4), 3, tb)
        shift = lax.rem(128 - off, 128)
        from_a = lane < 128 - off
        col = lane + (start + COLS * tx)
        col_in = (col >= 0) & (col < 2 * COLS)
        last = sec == N_SEC - 1
        s_list, d_list, m_list = ([], [], [])
        for m in range(NM):
            rows = pl.ds(m, 8, stride=NM)
            oa = own[ta, rows, :]
            ob = own[tb, rows, :]
            na = jnp.where(last, oa, nxt[ta, rows, :])
            nb = jnp.where(last, ob, nxt[tb, rows, :])
            row = row0 + m
            inside = (row >= 0) & (row < ROWS * n_ty) & col_in
            s_m = jnp.where(
                from_a, pltpu.roll(oa + na, shift, axis=1), pltpu.roll(ob + nb, shift, axis=1)
            )
            d_m = jnp.where(
                from_a, pltpu.roll(na - oa, shift, axis=1), pltpu.roll(nb - ob, shift, axis=1)
            )
            s_list.append(jnp.where(inside, s_m, 0.0))
            d_list.append(d_m)
            local = NM * sub + (m + HALO)
            tissue = ((local + lax.shift_right_logical(limit, 1)) & (ROWS - 1)) < limit
            m_list.append(jnp.where(tissue & col_in, 1.0, 0.0))
        for m in range(NM):
            up = s_list[m - 1] if m else pltpu.roll(s_list[NM - 1], 1, axis=0)
            down = s_list[m + 1] if m < NM - 1 else pltpu.roll(s_list[0], 7, axis=0)
            gx = 0.25 * (pltpu.roll(s_list[m], 127, axis=1) - pltpu.roll(s_list[m], 1, axis=1))
            gy = 0.25 * (down - up)
            gt = d_list[m]
            xx = gx * gx
            yy = gy * gy
            r = m_list[m] / (ALPHA + xx + yy)
            q = 0.25 * r
            coef[0, m] = (ALPHA + yy) * q
            coef[1, m] = gx * gy * q
            coef[2, m] = gx * gt * r
            coef[3, m] = (ALPHA + xx) * q
            coef[4, m] = gy * gt * r

        def around(x, m):
            up = x[m - 1] if m else pltpu.roll(x[NM - 1], 1, axis=0)
            down = x[m + 1] if m < NM - 1 else pltpu.roll(x[0], 7, axis=0)
            return (up + down) + (pltpu.roll(x[m], 1, axis=1) + pltpu.roll(x[m], 127, axis=1))

        def sweep(_, uv):
            u, v = (uv[:NM], uv[NM:])
            new_u, new_v = ([], [])
            for m in range(NM):
                mu = around(u, m)
                mv = around(v, m)
                b = coef[1, m]
                new_u.append(coef[0, m] * mu - b * mv - coef[2, m])
                new_v.append(coef[3, m] * mv - b * mu - coef[4, m])
            return tuple(new_u + new_v)

        first = [-coef[2, m] for m in range(NM)] + [-coef[4, m] for m in range(NM)]
        uv = lax.fori_loop(0, SWEEPS - 1, sweep, tuple(first))
        for c in range(2):
            for p in range(4):
                f = uv[16 * c + 4 * p : 16 * c + 4 * p + 4]
                pooled[pl.ds(8 * (4 * c + p), 8), pl.ds(pl.multiple_of(128 * j, 128), 128)] = (
                    f[0] + f[1]
                ) + (f[2] + f[3])
            for m in range(NM):
                flow[c, j, m] = uv[16 * c + m]
        return carry

    lax.fori_loop(0, TILES, tile_body, 0)

    coarse = dot3(pooled[...], pool_w[...])
    crow = 4 * sub + (16 * ty - 8)
    cmask = []
    for p in range(4):
        row_in = (crow + p >= 0) & (crow + p < 16 * n_ty)
        per_tile = []
        for t in range(2):
            q = lane + (128 * tx + (-8 if t == 0 else 104))
            per_tile.append(jnp.where(row_in & (q >= 0) & (q < 256), 1.0, 0.0))
        cmask.append(per_tile)
    e = [
        [[coarse[8 * (4 * c + p) : 8 * (4 * c + p) + 8, 128 * t : 128 * t + 128] for p in range(4)] for t in range(2)]
        for c in range(2)
    ]

    def mesh_sweep(x, t):
        out = []
        for p in range(4):
            up = x[p - 1] if p else pltpu.roll(x[3], 1, axis=0)
            down = x[p + 1] if p < 3 else pltpu.roll(x[0], 7, axis=0)
            total = (up + down) + (pltpu.roll(x[p], 1, axis=1) + pltpu.roll(x[p], 127, axis=1))
            out.append(total * cmask[p][t])
        return out

    def pack(e):
        out = []
        for p in range(4):
            both = [
                jnp.where(lane < 116, pltpu.roll(e[c][0][p], 120, axis=1), pltpu.roll(e[c][1][p], 104, axis=1))
                for c in range(2)
            ]
            out.append(jnp.where(sub < 4, pltpu.roll(both[0], 6, axis=0), pltpu.roll(both[1], 2, axis=0)))
        return out

    terms = [pack(e)]
    for _ in range(RELAX):
        e = [[mesh_sweep(e[c][t], t) for t in range(2)] for c in range(2)]
        terms.append(pack(e))
    base = sec * (N_SEC * (RELAX + 1))

    def combine(d):
        out = []
        for p in range(4):
            total = table_ref[base + d * (RELAX + 1)] * terms[0][p]
            for b in range(1, RELAX + 1):
                total = total + table_ref[base + d * (RELAX + 1) + b] * terms[b][p]
            out.append(total)
        return out

    shifts = (2, 1, 3)
    for d in shifts:
        for p, x in enumerate(combine(d)):
            sent[d - 1, p] = x
    mine = combine(0)
    exchanges = []
    for d in shifts:
        copy = pltpu.make_async_remote_copy(
            src_ref=sent.at[d - 1], dst_ref=got.at[d - 1],
            send_sem=csend_sem.at[d - 1], recv_sem=crecv_sem.at[d - 1],
            device_id=others[d - 1], device_id_type=MESH,
        )
        copy.start()
        exchanges.append(copy)

    for i in range(4):
        sh1 = jnp.where(tx == 0, 127 - 24 * i, 24 * i + 1)
        sh2 = jnp.where(tx == 0, 103 - 24 * i, 25 + 24 * i)
        take = jnp.where(tx == 0, lane, 127 - lane) < 115 - 24 * i

        def gather(m, carry, i=i, sh1=sh1, sh2=sh2, take=take):
            def both(j):
                return jnp.where(
                    sub < 4, pltpu.roll(flow[0, j, m], 6, axis=0), pltpu.roll(flow[1, j, m], 2, axis=0)
                )

            packed[i, m] = jnp.where(
                take, pltpu.roll(both(i), sh1, axis=1), pltpu.roll(both(i + 1), sh2, axis=1)
            )
            return carry

        lax.fori_loop(0, NM, gather, 0)

    for copy in exchanges:
        copy.wait_recv()
    disp = [((mine[p] + got[0, p]) + (got[1, p] + got[2, p])) for p in range(4)]
    back = dot3(jnp.concatenate(disp, axis=0), up_w[...])
    outs = []
    for i in range(4):
        a = jnp.where(tx == 0, i, 3 - i)
        for m in range(NM):
            p = m // 4
            local = NM * (sub & 3) + m
            tissue = ((local + lax.shift_right_logical(k_own, 1)) & (ROWS - 1)) < k_own
            value = packed[i, m] + jnp.where(tissue, back[8 * p : 8 * p + 8, 128 * i : 128 * i + 128], 0.0)
            outbuf[i, pl.ds(m, 8, stride=NM), :] = value
        for c in range(2):
            copy = pltpu.make_async_copy(
                outbuf.at[i, pl.ds(ROWS * c, ROWS), :],
                out_ref.at[c, 0, :, pl.ds(pl.multiple_of(128 * a, 128), 128)],
                out_sem.at[2 * i + c],
            )
            copy.start()
            outs.append(copy)
    for copy in copies:
        copy.wait_send()
    for copy in exchanges:
        copy.wait_send()
    for copy in outs:
        copy.wait()


def shards(images, tissue_rows, table):
    vmem = pltpu.VMEM
    return pl.pallas_call(
        kernel,
        out_shape=jax.ShapeDtypeStruct((2, 1, ROWS, COLS), F32),
        in_specs=[
            pl.BlockSpec(memory_space=pltpu.SMEM),
            pl.BlockSpec(memory_space=pltpu.SMEM),
            pl.BlockSpec(memory_space=pl.ANY),
        ],
        out_specs=pl.BlockSpec(memory_space=pl.ANY),
        scratch_shapes=[
            vmem((TILES, EXT, 128), F32),
            vmem((TILES, EXT, 128), F32),
            vmem((5, NM, 8, 128), F32),
            vmem((2, TILES, NM, 8, 128), F32),
            vmem((64, TILES * 128), F32),
            vmem((TILES * 128, 256), BF16),
            vmem((128, COLS), BF16),
            vmem((3, 4, 8, 128), F32),
            vmem((3, 4, 8, 128), F32),
            vmem((4, NM, 8, 128), F32),
            vmem((4, EXT, 128), F32),
            pltpu.SemaphoreType.DMA((4,)),
            pltpu.SemaphoreType.DMA((13,)),
            pltpu.SemaphoreType.DMA((13,)),
            pltpu.SemaphoreType.DMA((3,)),
            pltpu.SemaphoreType.DMA((3,)),
            pltpu.SemaphoreType.DMA((8,)),
        ],
        compiler_params=pltpu.CompilerParams(
            collective_id=0, has_side_effects=True, vmem_limit_bytes=16 * 1024 * 1024
        ),
        name="align",
    )(tissue_rows, table, images)


def solution(mesh):
    placed = (P("sec", "ty", "tx"), P(), P())
    mapped = jax.shard_map(
        shards, mesh=mesh, in_specs=placed, out_specs=P(None, "sec", "ty", "tx"), check_vma=False
    )

    def run(images, tissue_rows):
        return mapped(images, tissue_rows, jnp.asarray(section_table()))

    return run
```

time: 468 us -> 35.7 us (0.08)
  the two profiles are of different devices: /device:TPU:127 before, /device:TPU:24 now
where the time goes in v1:
time: 35.7 us; the launch traced here: 35.6 us
  Pallas kernels  32.7 us (92%)
  local copies, waits for them, and re-layouts  2.92 us (8%)
    pallas_call x1, Pallas kernels, shards(): pl.pallas_call(kernel, out_shape=jax.ShapeDtypeStruct((2, 1, ROWS, COLS),...  32.7 us
    unnamed x7, local copies, waits for them, and re-layouts  2.92 us

profile of v1, /device:TPU:24, one launch (start us, length us, event | category | flops | bytes accessed | tf_op | source)
XLA Modules:
  0.0 35.6 jit_solution(9052944708416588184)
XLA Ops:
  0.0 0.0 copy-start
  0.0 0.9 %copy-done = f32[1,64,512]{2,1,0:T(8,128)S(1)} copy-done((f32[1,64,512]{2,1,0:T(8,128)S(1)}, f32[1,64,512]{2,1,0:T(8,128)}, u32[]{:S(2)}) %copy-start) | copy-done | bytes 131096
  0.9 0.0 copy-start.1
  0.9 0.7 %copy-done.1 = s32[32]{0:T(128)S(1)} copy-done((s32[32]{0:T(128)S(1)}, s32[32]{0:T(128)}, u32[]{:S(2)}) %copy-start.1) | copy-done | bytes 152
  1.6 0.0 copy-start.2
  1.6 0.7 %copy-done.2 = f32[80]{0:T(128)S(1)} copy-done((f32[80]{0:T(128)S(1)}, f32[80]{0:T(128)}, u32[]{:S(2)}) %copy-start.2) | copy-done | bytes 344
  2.2 32.7 %align.1 = f32[2,1,64,512]{3,2,1,0:T(8,128)S(1)} custom-call(s32[32]{0:T(128)S(1)} %copy-done.1, f32[80]{0:T(128)S(1)} %copy-done.2, f32[1,64,512]{2,1,0:T(8,128)S(1)} %copy-done), custom_call_target="tpu_custom_call" | custom-call | tf_op jit(solution)/shard_map/align/pallas_call | solution.py:360
  34.9 0.7 %copy.5 = f32[2,1,64,512]{3,2,1,0:T(8,128)} copy(f32[2,1,64,512]{3,2,1,0:T(8,128)S(1)} %align.1) | data formatting | bytes 524288
Async XLA Ops:
  0.0 0.9 %copy-start = (f32[1,64,512]{2,1,0:T(8,128)S(1)}, f32[1,64,512]{2,1,0:T(8,128)}, u32[]{:S(2)}) copy-start(f32[1,64,512]{2,1,0:T(8,128)} %img_ref.1) | copy-start | bytes 393220
  0.9 0.7 %copy-start.1 = (s32[32]{0:T(128)S(1)}, s32[32]{0:T(128)}, u32[]{:S(2)}) copy-start(s32[32]{0:T(128)} %tissue_ref.1) | copy-start | bytes 388
  1.6 0.7 %copy-start.2 = (f32[80]{0:T(128)S(1)}, f32[80]{0:T(128)}, u32[]{:S(2)}) copy-start(f32[80]{0:T(128)} %constant.2.clone.table_ref) | copy-start | bytes 964

commit v2 on v1

v2 whole, which is shorter than its diff:
```python
import functools

import jax
import jax.numpy as jnp
import numpy as np
from jax import lax
from jax.experimental import pallas as pl
from jax.experimental.pallas import tpu as pltpu
from jax.sharding import PartitionSpec as P

MESH = pl.DeviceIdType.MESH
F32 = jnp.float32
BF16 = jnp.bfloat16

SWEEPS = 12
RELAX = 4
ALPHA = 0.5
STACK = 1.0
COUPLE = 0.5
TOTAL = 5.0

N_SEC = 4
ROWS = 64
COLS = 512
HALO = 32
EXT = ROWS + 2 * HALO
NM = EXT // 8
TILES = 5
STEP = 104


def section_table():
    w = {(0, 0): 1.0}
    for _ in range(RELAX):
        new = {(0, 0): 1.0}
        for (a, b), value in w.items():
            new[(a + 1, b)] = new.get((a + 1, b), 0.0) + value
            new[(a, b + 1)] = new.get((a, b + 1), 0.0) + value
        w = {key: value / TOTAL for key, value in new.items()}
    path = np.zeros((N_SEC, N_SEC))
    for i in range(N_SEC - 1):
        path[i, i + 1] = path[i + 1, i] = STACK
    table = np.zeros((N_SEC, N_SEC, RELAX + 1))
    for (a, b), value in w.items():
        power = np.linalg.matrix_power(path, a)
        for src in range(N_SEC):
            for shift in range(N_SEC):
                table[src, shift, b] += value * power[(src + shift) % N_SEC, src] * COUPLE**b
    return table.astype(np.float32)


TABLE = section_table()


def split3(x):
    hi = x.astype(BF16)
    rest = x - hi.astype(F32)
    mid = rest.astype(BF16)
    low = (rest - mid.astype(F32)).astype(BF16)
    return jnp.concatenate([hi, mid, low], axis=0)


def dot3(x, w):
    n = x.shape[0]
    y = jnp.dot(split3(x), w, preferred_element_type=F32)
    return y[:n] + y[n : 2 * n] + y[2 * n :]


def kernel(
    tissue_hbm, img_ref, out_ref,
    own, nxt, coef, fa, fb, pooled, pool_w, up_w, sent, got, packed, tissue_ref,
    load_sem, send_sem, recv_sem, csend_sem, crecv_sem,
):
    n_ty = lax.axis_size("ty")
    sec = lax.axis_index("sec")
    ty = lax.axis_index("ty")
    tx = lax.axis_index("tx")
    has_before, has_after = (ty > 0, ty < n_ty - 1)
    has_next, has_prev = (sec < N_SEC - 1, sec > 0)
    ty_b, ty_a = (jnp.maximum(ty - 1, 0), jnp.minimum(ty + 1, n_ty - 1))
    sec_n, sec_p = (jnp.minimum(sec + 1, N_SEC - 1), jnp.maximum(sec - 1, 0))
    partner = {"tx": 1 - tx}
    others = [{"sec": (sec + d) & (N_SEC - 1)} for d in range(1, N_SEC)]
    top, mid, low = (pl.ds(HALO, HALO), pl.ds(HALO, ROWS), pl.ds(ROWS, HALO))
    head, tail = (pl.ds(0, HALO), pl.ds(HALO + ROWS, HALO))
    four = pl.ds(0, 4)

    loads = [
        pltpu.make_async_copy(img_ref.at[0, :, pl.ds(128 * j, 128)], own.at[j, mid], load_sem.at[j])
        for j in range(4)
    ]
    for load in loads:
        load.start()
    tissue_load = pltpu.make_async_copy(tissue_hbm, tissue_ref, load_sem.at[4])
    tissue_load.start()

    barrier = pltpu.get_barrier_semaphore()
    meets = [(None, partner)] + [(None, d) for d in others]
    meets += [(has_before, {"ty": ty_b}), (has_after, {"ty": ty_a})]
    for has_sec, s_at in ((has_next, sec_n), (has_prev, sec_p)):
        meets += [
            (has_sec & has_before, {"sec": s_at, "ty": ty_b}),
            (has_sec & has_after, {"sec": s_at, "ty": ty_a}),
        ]

    def when(cond, fn):
        if cond is None:
            fn()
        else:
            pl.when(cond)(fn)

    n_meets = 0
    for cond, device in meets:
        when(cond, lambda device=device: pl.semaphore_signal(barrier, inc=1, device_id=device, device_id_type=MESH))
        n_meets = n_meets + (1 if cond is None else cond.astype(jnp.int32))

    lane = lax.broadcasted_iota(jnp.int32, (8, 128), 1)
    sub = lax.broadcasted_iota(jnp.int32, (8, 128), 0)

    def start_of(j):
        return jnp.where(tx == 0, STEP * j - 1, 385 - STEP * j)

    def clear(rows):
        def body():
            for ref in (own, nxt):
                for j in range(TILES):
                    ref[j, rows, :] = jnp.zeros((HALO, 128), F32)
        return body

    n_id = lax.broadcasted_iota(jnp.int32, (128, 256), 1)
    k_id = lax.broadcasted_iota(jnp.int32, (128, 256), 0)
    q_of = jnp.where(n_id < 128, n_id - 8, n_id - 24)
    for j in range(TILES):
        col = k_id + start_of(j)
        lo, hi = (12, 115)
        if j == 0:
            lo = jnp.where(tx == 0, 1, 12)
            hi = jnp.where(tx == 0, 115, 126)
        hit = (k_id >= lo) & (k_id <= hi) & (lax.shift_right_arithmetic(col, 2) == q_of)
        pool_w[pl.ds(128 * j, 128), :] = jnp.where(hit, 0.0625, 0.0).astype(BF16)
    un = lax.broadcasted_iota(jnp.int32, (128, 128), 1)
    uq = lax.broadcasted_iota(jnp.int32, (128, 128), 0)
    for i in range(4):
        a = jnp.where(tx == 0, i, 3 - i)
        hit = lax.shift_right_arithmetic(un + 128 * a, 2) == uq
        up_w[:, pl.ds(128 * i, 128)] = jnp.where(hit, 1.0, 0.0).astype(BF16)
    pl.when(jnp.logical_not(has_before))(clear(head))
    pl.when(jnp.logical_not(has_after))(clear(tail))

    for load in loads:
        load.wait()
    tissue_load.wait()
    pl.semaphore_wait(barrier, n_meets)

    edge = jnp.where(tx == 0, 3, 0)

    def remote(k, src, dst, device):
        return pltpu.make_async_remote_copy(
            src_ref=src, dst_ref=dst, send_sem=send_sem.at[k], recv_sem=recv_sem.at[k],
            device_id=device, device_id_type=MESH,
        )

    up_b, dn_a = (has_before, has_after)
    corner_t = (remote(0, own.at[four, top], nxt.at[four, tail], {"sec": sec_p, "ty": ty_b}), has_prev & up_b, has_next & dn_a)
    corner_h = (remote(1, own.at[four, low], nxt.at[four, head], {"sec": sec_p, "ty": ty_a}), has_prev & dn_a, has_next & up_b)
    next_mid = (remote(2, own.at[four, mid], nxt.at[four, mid], {"sec": sec_p}), has_prev, has_next)
    own_t = (remote(3, own.at[four, top], own.at[four, tail], {"ty": ty_b}), up_b, dn_a)
    own_h = (remote(4, own.at[four, low], own.at[four, head], {"ty": ty_a}), dn_a, up_b)
    side = (remote(5, own.at[edge, mid], own.at[4, mid], partner), None, None)
    side_ot = (remote(6, own.at[edge, tail], own.at[4, tail], partner), dn_a, dn_a)
    side_oh = (remote(7, own.at[edge, head], own.at[4, head], partner), up_b, up_b)
    side_m = (remote(8, nxt.at[edge, mid], nxt.at[4, mid], partner), has_next, has_next)
    side_t = (remote(9, nxt.at[edge, tail], nxt.at[4, tail], partner), has_next & dn_a, has_next & dn_a)
    side_h = (remote(10, nxt.at[edge, head], nxt.at[4, head], partner), has_next & up_b, has_next & up_b)
    copies = [corner_t, corner_h, next_mid, own_t, own_h, side, side_ot, side_oh, side_m, side_t, side_h]

    for copy, sends, _ in copies[:6]:
        when(sends, copy.start)
    for first, second in ((own_t, side_ot), (own_h, side_oh), (corner_t, side_t), (corner_h, side_h), (next_mid, side_m)):
        when(first[2], first[0].wait_recv)
        when(second[1], second[0].start)

    k_own = tissue_ref[ty]
    k_before = jnp.where(has_before, tissue_ref[ty_b], 0)
    k_after = jnp.where(has_after, tissue_ref[ty_a], 0)
    limit = jnp.where(sub < 2, k_before, jnp.where(sub < 6, k_own, k_after))
    half = lax.shift_right_logical(limit, 1)
    row0 = NM * sub + (ROWS * ty - HALO)
    last = jnp.logical_not(has_next)

    def shifted(x, m):
        up = x[m - 1] if m else pltpu.roll(x[NM - 1], 1, axis=0)
        down = x[m + 1] if m < NM - 1 else pltpu.roll(x[0], 7, axis=0)
        return up, down

    def coefficients(j, carry):
        @pl.when(j == 4)
        def _():
            for copy, _, receives in copies[5:]:
                when(receives, copy.wait_recv)

        start = start_of(j)
        pos = jnp.where(start < 0, start + 640, start)
        ta = lax.shift_right_logical(pos, 7)
        off = pos & 127
        tb = jnp.where(ta == 4, 0, ta + 1)
        ta = jnp.where((j == 0) & (ta == 4), 0, ta)
        tb = jnp.where((j == 0) & (tb == 4), 3, tb)
        shift = (128 - off) & 127
        from_a = lane < 128 - off
        col = lane + (start + COLS * tx)
        col_in = (col >= 0) & (col < 2 * COLS)
        s_list, d_list, m_list = ([], [], [])
        for m in range(NM):
            rows = pl.ds(m, 8, stride=NM)
            oa = own[ta, rows, :]
            ob = own[tb, rows, :]
            na = jnp.where(last, oa, nxt[ta, rows, :])
            nb = jnp.where(last, ob, nxt[tb, rows, :])
            row = row0 + m
            inside = (row >= 0) & (row < ROWS * n_ty) & col_in
            s_m = jnp.where(
                from_a, pltpu.roll(oa + na, shift, axis=1), pltpu.roll(ob + nb, shift, axis=1)
            )
            d_m = jnp.where(
                from_a, pltpu.roll(na - oa, shift, axis=1), pltpu.roll(nb - ob, shift, axis=1)
            )
            s_list.append(jnp.where(inside, s_m, 0.0))
            d_list.append(d_m)
            local = NM * sub + (m + HALO)
            tissue = ((local + half) & (ROWS - 1)) < limit
            m_list.append(jnp.where(tissue & col_in, 1.0, 0.0))
        for m in range(NM):
            up, down = shifted(s_list, m)
            gx = 0.25 * (pltpu.roll(s_list[m], 127, axis=1) - pltpu.roll(s_list[m], 1, axis=1))
            gy = 0.25 * (down - up)
            gt = d_list[m]
            xx = gx * gx
            yy = gy * gy
            r = m_list[m] / (ALPHA + xx + yy)
            q = 0.25 * r
            rt = gt * r
            coef[0, j, m] = (ALPHA + yy) * q
            coef[1, j, m] = gx * gy * q
            coef[2, j, m] = -(gx * rt)
            coef[3, j, m] = (ALPHA + xx) * q
            coef[4, j, m] = -(gy * rt)
        return carry

    lax.fori_loop(0, TILES, coefficients, 0)

    def sweep(read, dst):
        for j in range(TILES):
            u = [read(0, j, m) for m in range(NM)]
            v = [read(1, j, m) for m in range(NM)]
            for m in range(NM):
                means = []
                for x in (u, v):
                    up, down = shifted(x, m)
                    means.append((up + down) + (pltpu.roll(x[m], 1, axis=1) + pltpu.roll(x[m], 127, axis=1)))
                mu, mv = means
                b = coef[1, j, m]
                dst[0, j, m] = (coef[0, j, m] * mu - b * mv) + coef[2, j, m]
                dst[1, j, m] = (coef[3, j, m] * mv - b * mu) + coef[4, j, m]

    def of(ref):
        return lambda c, j, m: ref[c, j, m]

    sweep(lambda c, j, m: coef[2 + 2 * c, j, m], fa)

    def two_sweeps(_, carry):
        sweep(of(fa), fb)
        sweep(of(fb), fa)
        return carry

    lax.fori_loop(0, (SWEEPS - 2) // 2, two_sweeps, 0)

    for c in range(2):
        for p in range(4):
            for j in range(TILES):
                f = [fa[c, j, 4 * p + k] for k in range(4)]
                pooled[pl.ds(8 * (4 * c + p), 8), pl.ds(128 * j, 128)] = (f[0] + f[1]) + (f[2] + f[3])

    coarse = dot3(pooled[...], pool_w[...])
    crow = 4 * sub + (16 * ty - 8)
    cmask = []
    for p in range(4):
        row_in = (crow + p >= 0) & (crow + p < 16 * n_ty)
        per_tile = []
        for t in range(2):
            q = lane + (128 * tx + (-8 if t == 0 else 104))
            per_tile.append(jnp.where(row_in & (q >= 0) & (q < 256), 1.0, 0.0))
        cmask.append(per_tile)
    e = [
        [[coarse[8 * (4 * c + p) : 8 * (4 * c + p) + 8, 128 * t : 128 * t + 128] for p in range(4)] for t in range(2)]
        for c in range(2)
    ]

    def mesh_sweep(x, t):
        out = []
        for p in range(4):
            up = x[p - 1] if p else pltpu.roll(x[3], 1, axis=0)
            down = x[p + 1] if p < 3 else pltpu.roll(x[0], 7, axis=0)
            total = (up + down) + (pltpu.roll(x[p], 1, axis=1) + pltpu.roll(x[p], 127, axis=1))
            out.append(total * cmask[p][t])
        return out

    def pack(e):
        out = []
        for p in range(4):
            both = [
                jnp.where(lane < 116, pltpu.roll(e[c][0][p], 120, axis=1), pltpu.roll(e[c][1][p], 104, axis=1))
                for c in range(2)
            ]
            out.append(jnp.where(sub < 4, pltpu.roll(both[0], 6, axis=0), pltpu.roll(both[1], 2, axis=0)))
        return out

    terms = [pack(e)]
    for _ in range(RELAX):
        e = [[mesh_sweep(e[c][t], t) for t in range(2)] for c in range(2)]
        terms.append(pack(e))

    def weight(d, b):
        value = TABLE[N_SEC - 1, d, b]
        for src in range(N_SEC - 1):
            value = jnp.where(sec == src, TABLE[src, d, b], value)
        return value

    def combine(d):
        w = [weight(d, b) for b in range(RELAX + 1)]
        out = []
        for p in range(4):
            total = w[0] * terms[0][p]
            for b in range(1, RELAX + 1):
                total = total + w[b] * terms[b][p]
            out.append(total)
        return out

    shifts = (2, 1, 3)
    for d in shifts:
        for p, x in enumerate(combine(d)):
            sent[d - 1, p] = x
    mine = combine(0)
    exchanges = []
    for d in shifts:
        copy = pltpu.make_async_remote_copy(
            src_ref=sent.at[d - 1], dst_ref=got.at[d - 1],
            send_sem=csend_sem.at[d - 1], recv_sem=crecv_sem.at[d - 1],
            device_id=others[d - 1], device_id_type=MESH,
        )
        copy.start()
        exchanges.append(copy)

    shift_1 = [jnp.where(tx == 0, 127 - 24 * i, 24 * i + 1) for i in range(4)]
    shift_2 = [jnp.where(tx == 0, 103 - 24 * i, 25 + 24 * i) for i in range(4)]
    from_edge = jnp.where(tx == 0, lane, 127 - lane)
    for m in range(NM):
        both = [
            jnp.where(sub < 4, pltpu.roll(fa[0, j, m], 6, axis=0), pltpu.roll(fa[1, j, m], 2, axis=0))
            for j in range(TILES)
        ]
        for i in range(4):
            packed[i, m] = jnp.where(
                from_edge < 115 - 24 * i,
                pltpu.roll(both[i], shift_1[i], axis=1), pltpu.roll(both[i + 1], shift_2[i], axis=1),
            )
    for copy, sends, _ in copies:
        when(sends, copy.wait_send)

    for copy in exchanges:
        copy.wait_recv()
    disp = [((mine[p] + got[0, p]) + (got[1, p] + got[2, p])) for p in range(4)]
    back = dot3(jnp.concatenate(disp, axis=0), up_w[...])
    for m in range(NM):
        p = m // 4
        local = NM * (sub & 3) + m
        tissue = ((local + lax.shift_right_logical(k_own, 1)) & (ROWS - 1)) < k_own
        for i in range(4):
            a = jnp.where(tx == 0, i, 3 - i)
            value = packed[i, m] + jnp.where(tissue, back[8 * p : 8 * p + 8, 128 * i : 128 * i + 128], 0.0)
            out_ref[pl.ds((m // 8) * 32 + m % 8 + 8 * a, 8, stride=64), :] = value
    for copy in exchanges:
        copy.wait_send()


def shards(images, tissue_rows):
    vmem = pltpu.VMEM
    flat = pl.pallas_call(
        kernel,
        out_shape=jax.ShapeDtypeStruct((2 * ROWS * 4, 128), F32),
        in_specs=[pl.BlockSpec(memory_space=pltpu.HBM), pl.BlockSpec(memory_space=pltpu.HBM)],
        out_specs=pl.BlockSpec(memory_space=pltpu.VMEM),
        scratch_shapes=[
            vmem((TILES, EXT, 128), F32),
            vmem((TILES, EXT, 128), F32),
            vmem((5, TILES, NM, 8, 128), F32),
            vmem((2, TILES, NM, 8, 128), F32),
            vmem((2, TILES, NM, 8, 128), F32),
            vmem((64, TILES * 128), F32),
            vmem((TILES * 128, 256), BF16),
            vmem((128, COLS), BF16),
            vmem((3, 4, 8, 128), F32),
            vmem((3, 4, 8, 128), F32),
            vmem((4, NM, 8, 128), F32),
            pltpu.SMEM((32,), jnp.int32),
            pltpu.SemaphoreType.DMA((5,)),
            pltpu.SemaphoreType.DMA((11,)),
            pltpu.SemaphoreType.DMA((11,)),
            pltpu.SemaphoreType.DMA((3,)),
            pltpu.SemaphoreType.DMA((3,)),
        ],
        compiler_params=pltpu.CompilerParams(
            collective_id=0, has_side_effects=True, vmem_limit_bytes=24 * 1024 * 1024
        ),
        name="align",
    )(tissue_rows, images)
    tiles = flat.reshape(2, ROWS // 8, 4, 8, 128).transpose(0, 1, 3, 2, 4)
    return tiles.reshape(2, 1, ROWS, COLS)


def solution(mesh):
    return jax.shard_map(
        shards, mesh=mesh, in_specs=(P("sec", "ty", "tx"), P()), out_specs=P(None, "sec", "ty", "tx"), check_vma=False
    )
```

time: 35.7 us -> 23.9 us (0.67)
  the two profiles are of different devices: /device:TPU:24 before, /device:TPU:192 now
where the time goes in v2:
time: 23.9 us; the launch traced here: 23.8 us
  Pallas kernels  21.6 us (90%)
  local copies, waits for them, and re-layouts  2.26 us (9%)
    pallas_call x1, Pallas kernels, shards(): pl.pallas_call(kernel, out_shape=jax.ShapeDtypeStruct((2 * ROWS * 4, 128)...  21.6 us
    unnamed x5, local copies, waits for them, and re-layouts  2.26 us

profile of v2, /device:TPU:192, one launch (start us, length us, event | category | flops | bytes accessed | tf_op | source)
XLA Modules:
  0.0 23.8 jit_solution(9403468183481236806)
XLA Ops:
  0.0 0.0 copy-start
  0.0 0.9 %copy-done = f32[1,64,512]{2,1,0:T(8,128)S(1)} copy-done((f32[1,64,512]{2,1,0:T(8,128)S(1)}, f32[1,64,512]{2,1,0:T(8,128)}, u32[]{:S(2)}) %copy-start) | copy-done | bytes 131096
  0.9 0.0 copy-start.1
  0.9 0.7 %copy-done.1 = s32[32]{0:T(128)S(1)} copy-done((s32[32]{0:T(128)S(1)}, s32[32]{0:T(128)}, u32[]{:S(2)}) %copy-start.1) | copy-done | bytes 152
  1.6 21.6 %align.1 = f32[512,128]{1,0:T(8,128)S(1)} custom-call(s32[32]{0:T(128)S(1)} %copy-done.1, f32[1,64,512]{2,1,0:T(8,128)S(1)} %copy-done), custom_call_target="tpu_custom_call" | custom-call | tf_op jit(solution)/shard_map/align/pallas_call | solution.py:388
  23.1 0.7 %copy.4 = f32[2,1,64,512]{3,2,1,0:T(8,128)} copy(f32[2,1,64,512]{3,2,1,0:T(8,128)S(1)} %bitcast.5) | data formatting | bytes 524288
Async XLA Ops:
  0.0 0.9 %copy-start = (f32[1,64,512]{2,1,0:T(8,128)S(1)}, f32[1,64,512]{2,1,0:T(8,128)}, u32[]{:S(2)}) copy-start(f32[1,64,512]{2,1,0:T(8,128)} %img_ref.1) | copy-start | bytes 393220
  0.9 0.7 %copy-start.1 = (s32[32]{0:T(128)S(1)}, s32[32]{0:T(128)}, u32[]{:S(2)}) copy-start(s32[32]{0:T(128)} %tissue_hbm.1) | copy-start | bytes 388

commit v3 on v2

--- a/solution.py
+++ b/solution.py
@@ -68,7 +68,7 @@
 
 def kernel(
     tissue_hbm, img_ref, out_ref,
-    own, nxt, coef, fa, fb, pooled, pool_w, up_w, sent, got, packed, tissue_ref,
+    own, nxt, sbuf, tbuf, tmask, coef, x, pooled, pool_w, up_w, sent, got, packed, tissue_ref,
     load_sem, send_sem, recv_sem, csend_sem, crecv_sem,
 ):
     n_ty = lax.axis_size("ty")
@@ -147,9 +147,18 @@
     pl.when(jnp.logical_not(has_before))(clear(head))
     pl.when(jnp.logical_not(has_after))(clear(tail))
 
+    tissue_load.wait()
+    k_own = tissue_ref[ty]
+    k_before = jnp.where(has_before, tissue_ref[ty_b], 0)
+    k_after = jnp.where(has_after, tissue_ref[ty_a], 0)
+    limit = jnp.where(sub < 2, k_before, jnp.where(sub < 6, k_own, k_after))
+    half = lax.shift_right_logical(limit, 1)
+    for m in range(NM):
+        tmask[m] = jnp.where(((NM * sub + (m + HALO) + half) & (ROWS - 1)) < limit, 1.0, 0.0)
+    last = jnp.logical_not(has_next)
+
     for load in loads:
         load.wait()
-    tissue_load.wait()
     pl.semaphore_wait(barrier, n_meets)
 
     edge = jnp.where(tx == 0, 3, 0)
@@ -180,105 +189,109 @@
         when(first[2], first[0].wait_recv)
         when(second[1], second[0].start)
 
-    k_own = tissue_ref[ty]
-    k_before = jnp.where(has_before, tissue_ref[ty_b], 0)
-    k_after = jnp.where(has_after, tissue_ref[ty_a], 0)
-    limit = jnp.where(sub < 2, k_before, jnp.where(sub < 6, k_own, k_after))
-    half = lax.shift_right_logical(limit, 1)
-    row0 = NM * sub + (ROWS * ty - HALO)
-    last = jnp.logical_not(has_next)
-
-    def shifted(x, m):
-        up = x[m - 1] if m else pltpu.roll(x[NM - 1], 1, axis=0)
-        down = x[m + 1] if m < NM - 1 else pltpu.roll(x[0], 7, axis=0)
-        return up, down
-
-    def coefficients(j, carry):
-        @pl.when(j == 4)
-        def _():
-            for copy, _, receives in copies[5:]:
-                when(receives, copy.wait_recv)
-
-        start = start_of(j)
-        pos = jnp.where(start < 0, start + 640, start)
-        ta = lax.shift_right_logical(pos, 7)
-        off = pos & 127
-        tb = jnp.where(ta == 4, 0, ta + 1)
-        ta = jnp.where((j == 0) & (ta == 4), 0, ta)
-        tb = jnp.where((j == 0) & (tb == 4), 3, tb)
-        shift = (128 - off) & 127
-        from_a = lane < 128 - off
-        col = lane + (start + COLS * tx)
-        col_in = (col >= 0) & (col < 2 * COLS)
-        s_list, d_list, m_list = ([], [], [])
+    def build(tiles):
+        for side_of in range(2):
+            @pl.when(tx == side_of)
+            def _(side_of=side_of):
+                for j in tiles:
+                    start = STEP * j - 1 if side_of == 0 else 385 - STEP * j
+                    ta, off = ((start + 640) % 640 // 128, start % 128)
+                    tb = (ta + 1) % TILES
+                    if j == 0:
+                        ta, tb = (0, 0) if side_of == 0 else (3, 3)
+                    for m in range(NM):
+                        rows = pl.ds(m, 8, stride=NM)
+                        oa = own[ta, rows, :]
+                        ob = own[tb, rows, :]
+                        na = jnp.where(last, oa, nxt[ta, rows, :])
+                        nb = jnp.where(last, ob, nxt[tb, rows, :])
+                        shift = (m - off) % 128
+                        cc = (lane - m) & 127
+                        from_a = cc < 128 - off
+                        s_m, t_m = (
+                            jnp.where(from_a, pltpu.roll(ya, shift, axis=1), pltpu.roll(yb, shift, axis=1))
+                            for ya, yb in ((oa + na, ob + nb), (oa - na, ob - nb))
+                        )
+                        s_m = 0.25 * s_m
+                        if j == 0:
+                            s_m = jnp.where(cc >= 1 if side_of == 0 else cc < 127, s_m, 0.0)
+                        sbuf[j, m] = s_m
+                        tbuf[j, m] = t_m
+
+    lo, hi = (jnp.where(tx == 0, 1, 0), jnp.where(tx == 0, 128, 127))
+
+    def coefficients(j):
+        s_list = [sbuf[j, m] for m in range(NM)]
+        left = [pltpu.roll(v, 1, axis=1) for v in s_list]
+        right = [pltpu.roll(v, 127, axis=1) for v in s_list]
+        above = pltpu.roll(pltpu.roll(s_list[NM - 1], 1, axis=0), 113, axis=1)
+        below = pltpu.roll(pltpu.roll(s_list[0], 7, axis=0), 15, axis=1)
         for m in range(NM):
-            rows = pl.ds(m, 8, stride=NM)
-            oa = own[ta, rows, :]
-            ob = own[tb, rows, :]
-            na = jnp.where(last, oa, nxt[ta, rows, :])
-            nb = jnp.where(last, ob, nxt[tb, rows, :])
-            row = row0 + m
-            inside = (row >= 0) & (row < ROWS * n_ty) & col_in
-            s_m = jnp.where(
-                from_a, pltpu.roll(oa + na, shift, axis=1), pltpu.roll(ob + nb, shift, axis=1)
-            )
-            d_m = jnp.where(
-                from_a, pltpu.roll(na - oa, shift, axis=1), pltpu.roll(nb - ob, shift, axis=1)
-            )
-            s_list.append(jnp.where(inside, s_m, 0.0))
-            d_list.append(d_m)
-            local = NM * sub + (m + HALO)
-            tissue = ((local + half) & (ROWS - 1)) < limit
-            m_list.append(jnp.where(tissue & col_in, 1.0, 0.0))
-        for m in range(NM):
-            up, down = shifted(s_list, m)
-            gx = 0.25 * (pltpu.roll(s_list[m], 127, axis=1) - pltpu.roll(s_list[m], 1, axis=1))
-            gy = 0.25 * (down - up)
-            gt = d_list[m]
+            gx = right[m] - left[m]
+            gy = (right[m + 1] if m < NM - 1 else below) - (left[m - 1] if m else above)
+            mask = tmask[m]
+            if j == 0:
+                cc = (lane - m) & 127
+                mask = jnp.where((cc >= lo) & (cc < hi), mask, 0.0)
             xx = gx * gx
-            yy = gy * gy
-            r = m_list[m] / (ALPHA + xx + yy)
+            yy = ALPHA + gy * gy
+            r = mask / (xx + yy)
             q = 0.25 * r
-            rt = gt * r
-            coef[0, j, m] = (ALPHA + yy) * q
-            coef[1, j, m] = gx * gy * q
-            coef[2, j, m] = -(gx * rt)
-            coef[3, j, m] = (ALPHA + xx) * q
-            coef[4, j, m] = -(gy * rt)
+            rt = tbuf[j, m] * r
+            values = (yy * q, gx * gy * q, gx * rt, (ALPHA + xx) * q, gy * rt)
+            for k, value in enumerate(values):
+                if k not in (2, 4):
+                    coef[0, k, j, m] = value
+                    coef[1, k, j, m] = pltpu.roll(value, 1, axis=1)
+                else:
+                    moved = pltpu.roll(value, 1, axis=1)
+                    coef[0, k, j, m] = value
+                    coef[1, k, j, m] = moved
+                    x[k // 2 - 1, j, m] = moved
+
+    build(range(4))
+    for j in range(4):
+        coefficients(j)
+    for copy, _, receives in copies[5:]:
+        when(receives, copy.wait_recv)
+    build((4,))
+    coefficients(4)
+
+    def sweep(kind):
+        for j in range(TILES):
+            means = []
+            for c in range(2):
+                f = [x[c, j, m] for m in range(NM)]
+                below = pltpu.roll(f[0], 7, axis=0)
+                above = pltpu.roll(f[NM - 1], 1, axis=0)
+                g = [f[m] + f[m + 1] for m in range(NM - 1)]
+                if kind == 0:
+                    one = [pltpu.roll(y, 126, axis=1) for y in g]
+                    one.append(pltpu.roll(f[NM - 1], 126, axis=1) + pltpu.roll(below, 14, axis=1))
+                    two = [pltpu.roll(above, 112, axis=1) + f[0]] + g
+                else:
+                    one = g + [f[NM - 1] + pltpu.roll(below, 16, axis=1)]
+                    two = [pltpu.roll(above, 114, axis=1) + pltpu.roll(f[0], 2, axis=1)]
+                    two += [pltpu.roll(y, 2, axis=1) for y in g]
+                means.append([one[m] + two[m] for m in range(NM)])
+            for m in range(NM):
+                mu, mv = (means[0][m], means[1][m])
+                k = [coef[kind, i, j, m] for i in range(5)]
+                x[0, j, m] = (k[0] * mu - k[1] * mv) + k[2]
+                x[1, j, m] = (k[3] * mv - k[1] * mu) + k[4]
+
+    def two_sweeps(_, carry):
+        sweep(1)
+        sweep(0)
         return carry
 
-    lax.fori_loop(0, TILES, coefficients, 0)
-
-    def sweep(read, dst):
-        for j in range(TILES):
-            u = [read(0, j, m) for m in range(NM)]
-            v = [read(1, j, m) for m in range(NM)]
-            for m in range(NM):
-                means = []
-                for x in (u, v):
-                    up, down = shifted(x, m)
-                    means.append((up + down) + (pltpu.roll(x[m], 1, axis=1) + pltpu.roll(x[m], 127, axis=1)))
-                mu, mv = means
-                b = coef[1, j, m]
-                dst[0, j, m] = (coef[0, j, m] * mu - b * mv) + coef[2, j, m]
-                dst[1, j, m] = (coef[3, j, m] * mv - b * mu) + coef[4, j, m]
-
-    def of(ref):
-        return lambda c, j, m: ref[c, j, m]
-
-    sweep(lambda c, j, m: coef[2 + 2 * c, j, m], fa)
-
-    def two_sweeps(_, carry):
-        sweep(of(fa), fb)
-        sweep(of(fb), fa)
-        return carry
-
+    sweep(0)
     lax.fori_loop(0, (SWEEPS - 2) // 2, two_sweeps, 0)
 
-    for c in range(2):
-        for p in range(4):
-            for j in range(TILES):
-                f = [fa[c, j, 4 * p + k] for k in range(4)]
+    for j in range(TILES):
+        for c in range(2):
+            for p in range(4):
+                f = [pltpu.roll(x[c, j, m], (128 - m) & 127, axis=1) if m else x[c, j, m] for m in range(4 * p, 4 * p + 4)]
                 pooled[pl.ds(8 * (4 * c + p), 8), pl.ds(128 * j, 128)] = (f[0] + f[1]) + (f[2] + f[3])
 
     coarse = dot3(pooled[...], pool_w[...])
@@ -296,12 +309,12 @@
         for c in range(2)
     ]
 
-    def mesh_sweep(x, t):
+    def mesh_sweep(y, t):
         out = []
         for p in range(4):
-            up = x[p - 1] if p else pltpu.roll(x[3], 1, axis=0)
-            down = x[p + 1] if p < 3 else pltpu.roll(x[0], 7, axis=0)
-            total = (up + down) + (pltpu.roll(x[p], 1, axis=1) + pltpu.roll(x[p], 127, axis=1))
+            up = y[p - 1] if p else pltpu.roll(y[3], 1, axis=0)
+            down = y[p + 1] if p < 3 else pltpu.roll(y[0], 7, axis=0)
+            total = (up + down) + (pltpu.roll(y[p], 1, axis=1) + pltpu.roll(y[p], 127, axis=1))
             out.append(total * cmask[p][t])
         return out
 
@@ -338,8 +351,8 @@
 
     shifts = (2, 1, 3)
     for d in shifts:
-        for p, x in enumerate(combine(d)):
-            sent[d - 1, p] = x
+        for p, term in enumerate(combine(d)):
+            sent[d - 1, p] = term
     mine = combine(0)
     exchanges = []
     for d in shifts:
@@ -351,19 +364,22 @@
         copy.start()
         exchanges.append(copy)
 
-    shift_1 = [jnp.where(tx == 0, 127 - 24 * i, 24 * i + 1) for i in range(4)]
-    shift_2 = [jnp.where(tx == 0, 103 - 24 * i, 25 + 24 * i) for i in range(4)]
-    from_edge = jnp.where(tx == 0, lane, 127 - lane)
-    for m in range(NM):
-        both = [
-            jnp.where(sub < 4, pltpu.roll(fa[0, j, m], 6, axis=0), pltpu.roll(fa[1, j, m], 2, axis=0))
-            for j in range(TILES)
-        ]
-        for i in range(4):
-            packed[i, m] = jnp.where(
-                from_edge < 115 - 24 * i,
-                pltpu.roll(both[i], shift_1[i], axis=1), pltpu.roll(both[i + 1], shift_2[i], axis=1),
-            )
+    for side_of in range(2):
+        @pl.when(tx == side_of)
+        def _(side_of=side_of):
+            for m in range(NM):
+                both = [
+                    jnp.where(sub < 4, pltpu.roll(x[0, j, m], 6, axis=0), pltpu.roll(x[1, j, m], 2, axis=0))
+                    for j in range(TILES)
+                ]
+                for i in range(4):
+                    sh1, sh2 = (127 - 24 * i, 103 - 24 * i) if side_of == 0 else (24 * i + 1, 25 + 24 * i)
+                    from_edge = lane if side_of == 0 else 127 - lane
+                    packed[i, m] = jnp.where(
+                        from_edge < 115 - 24 * i,
+                        pltpu.roll(both[i], (sh1 - m) % 128, axis=1), pltpu.roll(both[i + 1], (sh2 - m) % 128, axis=1),
+                    )
+
     for copy, sends, _ in copies:
         when(sends, copy.wait_send)
 
@@ -393,8 +409,10 @@
         scratch_shapes=[
             vmem((TILES, EXT, 128), F32),
             vmem((TILES, EXT, 128), F32),
-            vmem((5, TILES, NM, 8, 128), F32),
-            vmem((2, TILES, NM, 8, 128), F32),
+            vmem((TILES, NM, 8, 128), F32),
+            vmem((TILES, NM, 8, 128), F32),
+            vmem((NM, 8, 128), F32),
+            vmem((2, 5, TILES, NM, 8, 128), F32),
             vmem((2, TILES, NM, 8, 128), F32),
             vmem((64, TILES * 128), F32),
             vmem((TILES * 128, 256), BF16),
@@ -413,7 +431,7 @@
             collective_id=0, has_side_effects=True, vmem_limit_bytes=24 * 1024 * 1024
         ),
         name="align",
-    )(tissue_rows, images)
+    )(*(pltpu.with_memory_space_constraint(y, pltpu.HBM) for y in (tissue_rows, images)))
     tiles = flat.reshape(2, ROWS // 8, 4, 8, 128).transpose(0, 1, 3, 2, 4)
     return tiles.reshape(2, 1, ROWS, COLS)
 

time: 23.9 us -> 21.3 us (0.89)
  local copies, waits for them, and re-layouts: 2.26 us -> 0.71 us
  Pallas kernels: 21.6 us -> 20.5 us
    unnamed x5 -> x1, local copies, waits for them, and re-layouts: 2.26 us -> 0.71 us
    pallas_call x1, Pallas kernels: 21.6 us -> 20.5 us  [shards(): pl.pallas_call(kernel, out_shape=jax.ShapeDtypeStruct((2 * ROWS * 4, 128)...]
where the time goes in v3:
time: 21.3 us; the launch traced here: 21.2 us
  Pallas kernels  20.5 us (96%)
  local copies, waits for them, and re-layouts  0.71 us (3%)
    pallas_call x1, Pallas kernels, shards(): pl.pallas_call(kernel, out_shape=jax.ShapeDtypeStruct((2 * ROWS * 4, 128)...  20.5 us
    unnamed x1, local copies, waits for them, and re-layouts  0.71 us

profile of v3, /device:TPU:192, one launch (start us, length us, event | category | flops | bytes accessed | tf_op | source)
XLA Modules:
  0.0 21.2 jit_solution(17946996798735676562)
XLA Ops:
  0.0 20.5 %align.1 = f32[512,128]{1,0:T(8,128)S(1)} custom-call(s32[32]{0:T(128)} %tissue_hbm.1, f32[1,64,512]{2,1,0:T(8,128)} %img_ref.1), custom_call_target="tpu_custom_call" | custom-call | tf_op jit(solution)/shard_map/align/pallas_call | solution.py:404
  20.5 0.7 %copy.4 = f32[2,1,64,512]{3,2,1,0:T(8,128)} copy(f32[2,1,64,512]{3,2,1,0:T(8,128)S(1)} %bitcast.5) | data formatting | bytes 524288

commit v4 on v3

--- a/solution.py
+++ b/solution.py
@@ -222,32 +222,30 @@
 
     def coefficients(j):
         s_list = [sbuf[j, m] for m in range(NM)]
-        left = [pltpu.roll(v, 1, axis=1) for v in s_list]
-        right = [pltpu.roll(v, 127, axis=1) for v in s_list]
-        above = pltpu.roll(pltpu.roll(s_list[NM - 1], 1, axis=0), 113, axis=1)
-        below = pltpu.roll(pltpu.roll(s_list[0], 7, axis=0), 15, axis=1)
-        for m in range(NM):
-            gx = right[m] - left[m]
-            gy = (right[m + 1] if m < NM - 1 else below) - (left[m - 1] if m else above)
-            mask = tmask[m]
-            if j == 0:
-                cc = (lane - m) & 127
-                mask = jnp.where((cc >= lo) & (cc < hi), mask, 0.0)
-            xx = gx * gx
-            yy = ALPHA + gy * gy
-            r = mask / (xx + yy)
-            q = 0.25 * r
-            rt = tbuf[j, m] * r
-            values = (yy * q, gx * gy * q, gx * rt, (ALPHA + xx) * q, gy * rt)
-            for k, value in enumerate(values):
-                if k not in (2, 4):
-                    coef[0, k, j, m] = value
-                    coef[1, k, j, m] = pltpu.roll(value, 1, axis=1)
-                else:
-                    moved = pltpu.roll(value, 1, axis=1)
-                    coef[0, k, j, m] = value
-                    coef[1, k, j, m] = moved
-                    x[k // 2 - 1, j, m] = moved
+        for frame in range(2):
+            left = [pltpu.roll(v, 1 + frame, axis=1) for v in s_list]
+            right = s_list if frame else [pltpu.roll(v, 127, axis=1) for v in s_list]
+            above = pltpu.roll(pltpu.roll(s_list[NM - 1], 1, axis=0), 113 + frame, axis=1)
+            below = pltpu.roll(pltpu.roll(s_list[0], 7, axis=0), 15 + frame, axis=1)
+            for m in range(NM):
+                gx = right[m] - left[m]
+                gy = (right[m + 1] if m < NM - 1 else below) - (left[m - 1] if m else above)
+                gt = pltpu.roll(tbuf[j, m], 1, axis=1) if frame else tbuf[j, m]
+                mask = tmask[m]
+                if j == 0:
+                    cc = (lane - (m + frame)) & 127
+                    mask = jnp.where((cc >= lo) & (cc < hi), mask, 0.0)
+                xx = gx * gx
+                yy = ALPHA + gy * gy
+                r = mask / (xx + yy)
+                q = 0.25 * r
+                rt = gt * r
+                values = (yy * q, gx * gy * q, gx * rt, (ALPHA + xx) * q, gy * rt)
+                for k, value in enumerate(values):
+                    coef[frame, k, j, m] = value
+                if frame:
+                    x[0, j, m] = values[2]
+                    x[1, j, m] = values[4]
 
     build(range(4))
     for j in range(4):

time: 21.3 us -> 20.9 us (0.981)
  Pallas kernels: 20.5 us -> 20 us
    pallas_call x1, Pallas kernels: 20.5 us -> 20 us  [shards(): pl.pallas_call(kernel, out_shape=jax.ShapeDtypeStruct((2 * ROWS * 4, 128)...]
where the time goes in v4:
time: 20.9 us; the launch traced here: 20.7 us
  Pallas kernels  20 us (96%)
  local copies, waits for them, and re-layouts  0.71 us (3%)
    pallas_call x1, Pallas kernels, shards(): pl.pallas_call(kernel, out_shape=jax.ShapeDtypeStruct((2 * ROWS * 4, 128)...  20 us
    unnamed x1, local copies, waits for them, and re-layouts  0.71 us

profile of v4, /device:TPU:192, one launch (start us, length us, event | category | flops | bytes accessed | tf_op | source)
XLA Modules:
  0.0 20.7 jit_solution(4331699295204541144)
XLA Ops:
  0.0 20.0 %align.1 = f32[512,128]{1,0:T(8,128)S(1)} custom-call(s32[32]{0:T(128)} %tissue_hbm.1, f32[1,64,512]{2,1,0:T(8,128)} %img_ref.1), custom_call_target="tpu_custom_call" | custom-call | tf_op jit(solution)/shard_map/align/pallas_call | solution.py:402
  20.0 0.7 %copy.4 = f32[2,1,64,512]{3,2,1,0:T(8,128)} copy(f32[2,1,64,512]{3,2,1,0:T(8,128)S(1)} %bitcast.5) | data formatting | bytes 524288

commit v5 on v4

--- a/solution.py
+++ b/solution.py
@@ -23,6 +23,7 @@
 ROWS = 64
 COLS = 512
 HALO = 32
+REACH = 29
 EXT = ROWS + 2 * HALO
 NM = EXT // 8
 TILES = 5
@@ -85,6 +86,32 @@
     head, tail = (pl.ds(0, HALO), pl.ds(HALO + ROWS, HALO))
     four = pl.ds(0, 4)
 
+    for ref in (own, nxt):
+        for j in range(4):
+            for at in (0, EXT - 8):
+                ref[j, pl.ds(at, 8), :] = jnp.zeros((8, 128), F32)
+
+    barrier = pltpu.get_barrier_semaphore()
+    meets = []
+    for has_sec, s_at in ((has_next, sec_n), (has_prev, sec_p)):
+        meets += [
+            (has_sec & has_before, {"sec": s_at, "ty": ty_b}),
+            (has_sec & has_after, {"sec": s_at, "ty": ty_a}),
+        ]
+    meets += [(has_before, {"ty": ty_b}), (has_after, {"ty": ty_a})]
+    meets += [(None, others[d]) for d in (1, 0, 2)] + [(None, partner)]
+
+    def when(cond, fn):
+        if cond is None:
+            fn()
+        else:
+            pl.when(cond)(fn)
+
+    n_meets = 0
+    for cond, device in meets:
+        when(cond, lambda device=device: pl.semaphore_signal(barrier, inc=1, device_id=device, device_id_type=MESH))
+        n_meets = n_meets + (1 if cond is None else cond.astype(jnp.int32))
+
     loads = [
         pltpu.make_async_copy(img_ref.at[0, :, pl.ds(128 * j, 128)], own.at[j, mid], load_sem.at[j])
         for j in range(4)
@@ -93,26 +120,6 @@
         load.start()
     tissue_load = pltpu.make_async_copy(tissue_hbm, tissue_ref, load_sem.at[4])
     tissue_load.start()
-
-    barrier = pltpu.get_barrier_semaphore()
-    meets = [(None, partner)] + [(None, d) for d in others]
-    meets += [(has_before, {"ty": ty_b}), (has_after, {"ty": ty_a})]
-    for has_sec, s_at in ((has_next, sec_n), (has_prev, sec_p)):
-        meets += [
-            (has_sec & has_before, {"sec": s_at, "ty": ty_b}),
-            (has_sec & has_after, {"sec": s_at, "ty": ty_a}),
-        ]
-
-    def when(cond, fn):
-        if cond is None:
-            fn()
-        else:
-            pl.when(cond)(fn)
-
-    n_meets = 0
-    for cond, device in meets:
-        when(cond, lambda device=device: pl.semaphore_signal(barrier, inc=1, device_id=device, device_id_type=MESH))
-        n_meets = n_meets + (1 if cond is None else cond.astype(jnp.int32))
 
     lane = lax.broadcasted_iota(jnp.int32, (8, 128), 1)
     sub = lax.broadcasted_iota(jnp.int32, (8, 128), 0)
@@ -170,11 +177,11 @@
         )
 
     up_b, dn_a = (has_before, has_after)
-    corner_t = (remote(0, own.at[four, top], nxt.at[four, tail], {"sec": sec_p, "ty": ty_b}), has_prev & up_b, has_next & dn_a)
-    corner_h = (remote(1, own.at[four, low], nxt.at[four, head], {"sec": sec_p, "ty": ty_a}), has_prev & dn_a, has_next & up_b)
+    corner_t = (remote(0, own.at[four, pl.ds(HALO, REACH)], nxt.at[four, pl.ds(HALO + ROWS, REACH)], {"sec": sec_p, "ty": ty_b}), has_prev & up_b, has_next & dn_a)
+    corner_h = (remote(1, own.at[four, pl.ds(HALO + ROWS - REACH, REACH)], nxt.at[four, pl.ds(HALO - REACH, REACH)], {"sec": sec_p, "ty": ty_a}), has_prev & dn_a, has_next & up_b)
     next_mid = (remote(2, own.at[four, mid], nxt.at[four, mid], {"sec": sec_p}), has_prev, has_next)
-    own_t = (remote(3, own.at[four, top], own.at[four, tail], {"ty": ty_b}), up_b, dn_a)
-    own_h = (remote(4, own.at[four, low], own.at[four, head], {"ty": ty_a}), dn_a, up_b)
+    own_t = (remote(3, own.at[four, pl.ds(HALO, REACH)], own.at[four, pl.ds(HALO + ROWS, REACH)], {"ty": ty_b}), up_b, dn_a)
+    own_h = (remote(4, own.at[four, pl.ds(HALO + ROWS - REACH, REACH)], own.at[four, pl.ds(HALO - REACH, REACH)], {"ty": ty_a}), dn_a, up_b)
     side = (remote(5, own.at[edge, mid], own.at[4, mid], partner), None, None)
     side_ot = (remote(6, own.at[edge, tail], own.at[4, tail], partner), dn_a, dn_a)
     side_oh = (remote(7, own.at[edge, head], own.at[4, head], partner), up_b, up_b)
@@ -284,7 +291,8 @@
         return carry
 
     sweep(0)
-    lax.fori_loop(0, (SWEEPS - 2) // 2, two_sweeps, 0)
+    for _ in range((SWEEPS - 2) // 2):
+        two_sweeps(0, 0)
 
     for j in range(TILES):
         for c in range(2):
@@ -326,10 +334,7 @@
             out.append(jnp.where(sub < 4, pltpu.roll(both[0], 6, axis=0), pltpu.roll(both[1], 2, axis=0)))
         return out
 
-    terms = [pack(e)]
-    for _ in range(RELAX):
-        e = [[mesh_sweep(e[c][t], t) for t in range(2)] for c in range(2)]
-        terms.append(pack(e))
+    terms = [e]
 
     def weight(d, b):
         value = TABLE[N_SEC - 1, d, b]
@@ -338,22 +343,24 @@
         return value
 
     def combine(d):
-        w = [weight(d, b) for b in range(RELAX + 1)]
-        out = []
-        for p in range(4):
-            total = w[0] * terms[0][p]
-            for b in range(1, RELAX + 1):
-                total = total + w[b] * terms[b][p]
-            out.append(total)
-        return out
-
-    shifts = (2, 1, 3)
-    for d in shifts:
+        total = None
+        for b in range(RELAX + 1):
+            if not TABLE[:, d, b].any():
+                continue
+            w = weight(d, b)
+            part = [[[w * y for y in terms[b][c][t]] for t in range(2)] for c in range(2)]
+            total = part if total is None else [
+                [[y + z for y, z in zip(total[c][t], part[c][t])] for t in range(2)] for c in range(2)
+            ]
+        return pack(total)
+
+    exchanges = []
+    for d in (2, 1, 3):
+        while any(TABLE[:, d, b].any() for b in range(len(terms), RELAX + 1)):
+            e = [[mesh_sweep(e[c][t], t) for t in range(2)] for c in range(2)]
+            terms.append(e)
         for p, term in enumerate(combine(d)):
             sent[d - 1, p] = term
-    mine = combine(0)
-    exchanges = []
-    for d in shifts:
         copy = pltpu.make_async_remote_copy(
             src_ref=sent.at[d - 1], dst_ref=got.at[d - 1],
             send_sem=csend_sem.at[d - 1], recv_sem=crecv_sem.at[d - 1],
@@ -361,6 +368,10 @@
         )
         copy.start()
         exchanges.append(copy)
+    while len(terms) <= RELAX:
+        e = [[mesh_sweep(e[c][t], t) for t in range(2)] for c in range(2)]
+        terms.append(e)
+    mine = combine(0)
 
     for side_of in range(2):
         @pl.when(tx == side_of)

time: 20.9 us -> 20.2 us (0.967)
  Pallas kernels: 20 us -> 19.3 us
    pallas_call x1, Pallas kernels: 20 us -> 19.3 us  [shards(): pl.pallas_call(kernel, out_shape=jax.ShapeDtypeStruct((2 * ROWS * 4, 128)...]
where the time goes in v5:
time: 20.2 us; the launch traced here: 20.1 us
  Pallas kernels  19.3 us (96%)
  local copies, waits for them, and re-layouts  0.71 us (4%)
    pallas_call x1, Pallas kernels, shards(): pl.pallas_call(kernel, out_shape=jax.ShapeDtypeStruct((2 * ROWS * 4, 128)...  19.3 us
    unnamed x1, local copies, waits for them, and re-layouts  0.71 us

profile of v5, /device:TPU:192, one launch (start us, length us, event | category | flops | bytes accessed | tf_op | source)
XLA Modules:
  0.0 20.1 jit_solution(8920093174422917851)
XLA Ops:
  0.0 19.3 %align.1 = f32[512,128]{1,0:T(8,128)S(1)} custom-call(s32[32]{0:T(128)} %tissue_hbm.1, f32[1,64,512]{2,1,0:T(8,128)} %img_ref.1), custom_call_target="tpu_custom_call" | custom-call | tf_op jit(solution)/shard_map/align/pallas_call | solution.py:413
  19.4 0.7 %copy.4 = f32[2,1,64,512]{3,2,1,0:T(8,128)} copy(f32[2,1,64,512]{3,2,1,0:T(8,128)S(1)} %bitcast.5) | data formatting | bytes 524288

commit v6 on v5

--- a/solution.py
+++ b/solution.py
@@ -192,11 +192,7 @@
 
     for copy, sends, _ in copies[:6]:
         when(sends, copy.start)
-    for first, second in ((own_t, side_ot), (own_h, side_oh), (corner_t, side_t), (corner_h, side_h), (next_mid, side_m)):
-        when(first[2], first[0].wait_recv)
-        when(second[1], second[0].start)
-
-    def build(tiles):
+    def build(tiles, ref):
         for side_of in range(2):
             @pl.when(tx == side_of)
             def _(side_of=side_of):
@@ -208,22 +204,29 @@
                         ta, tb = (0, 0) if side_of == 0 else (3, 3)
                     for m in range(NM):
                         rows = pl.ds(m, 8, stride=NM)
-                        oa = own[ta, rows, :]
-                        ob = own[tb, rows, :]
-                        na = jnp.where(last, oa, nxt[ta, rows, :])
-                        nb = jnp.where(last, ob, nxt[tb, rows, :])
                         shift = (m - off) % 128
                         cc = (lane - m) & 127
-                        from_a = cc < 128 - off
-                        s_m, t_m = (
-                            jnp.where(from_a, pltpu.roll(ya, shift, axis=1), pltpu.roll(yb, shift, axis=1))
-                            for ya, yb in ((oa + na, ob + nb), (oa - na, ob - nb))
+                        y = jnp.where(
+                            cc < 128 - off,
+                            pltpu.roll(ref[ta, rows, :], shift, axis=1), pltpu.roll(ref[tb, rows, :], shift, axis=1),
                         )
-                        s_m = 0.25 * s_m
+                        if ref is own:
+                            sbuf[j, m] = y
+                            continue
+                        o = sbuf[j, m]
+                        y = jnp.where(last, o, y)
+                        s_m = 0.25 * (o + y)
                         if j == 0:
                             s_m = jnp.where(cc >= 1 if side_of == 0 else cc < 127, s_m, 0.0)
                         sbuf[j, m] = s_m
-                        tbuf[j, m] = t_m
+                        tbuf[j, m] = o - y
+
+    for first, second in ((own_t, side_ot), (own_h, side_oh), (corner_t, side_t), (corner_h, side_h)):
+        when(first[2], first[0].wait_recv)
+        when(second[1], second[0].start)
+    build(range(4), own)
+    when(next_mid[2], next_mid[0].wait_recv)
+    when(side_m[1], side_m[0].start)
 
     lo, hi = (jnp.where(tx == 0, 1, 0), jnp.where(tx == 0, 128, 127))
 
@@ -254,12 +257,15 @@
                     x[0, j, m] = values[2]
                     x[1, j, m] = values[4]
 
-    build(range(4))
+    build(range(4), nxt)
     for j in range(4):
         coefficients(j)
-    for copy, _, receives in copies[5:]:
+    for copy, _, receives in (side, side_ot, side_oh):
         when(receives, copy.wait_recv)
-    build((4,))
+    build((4,), own)
+    for copy, _, receives in (side_m, side_t, side_h):
+        when(receives, copy.wait_recv)
+    build((4,), nxt)
     coefficients(4)
 
     def sweep(kind):

time: 20.2 us -> 20.1 us (level)
  no operation moved by 1% of the time
where the time goes in v6:
time: 20.1 us; the launch traced here: 20 us
  Pallas kernels  19.3 us (96%)
  local copies, waits for them, and re-layouts  0.71 us (4%)
    pallas_call x1, Pallas kernels, shards(): pl.pallas_call(kernel, out_shape=jax.ShapeDtypeStruct((2 * ROWS * 4, 128)...  19.3 us
    unnamed x1, local copies, waits for them, and re-layouts  0.71 us

profile of v6, /device:TPU:192, one launch (start us, length us, event | category | flops | bytes accessed | tf_op | source)
XLA Modules:
  0.0 20.0 jit_solution(10247585842176047026)
XLA Ops:
  0.0 19.3 %align.1 = f32[512,128]{1,0:T(8,128)S(1)} custom-call(s32[32]{0:T(128)} %tissue_hbm.1, f32[1,64,512]{2,1,0:T(8,128)} %img_ref.1), custom_call_target="tpu_custom_call" | custom-call | tf_op jit(solution)/shard_map/align/pallas_call | solution.py:419
  19.3 0.7 %copy.4 = f32[2,1,64,512]{3,2,1,0:T(8,128)} copy(f32[2,1,64,512]{3,2,1,0:T(8,128)S(1)} %bitcast.5) | data formatting | bytes 524288

commit v7 on v6

--- a/solution.py
+++ b/solution.py
@@ -69,7 +69,7 @@
 
 def kernel(
     tissue_hbm, img_ref, out_ref,
-    own, nxt, sbuf, tbuf, tmask, coef, x, pooled, pool_w, up_w, sent, got, packed, tissue_ref,
+    own, nxt, sbuf, tbuf, tmask, coef, x, pooled, pool_w, up_w, sent, got, back, tissue_ref,
     load_sem, send_sem, recv_sem, csend_sem, crecv_sem,
 ):
     n_ty = lax.axis_size("ty")
@@ -390,7 +390,8 @@
                 for i in range(4):
                     sh1, sh2 = (127 - 24 * i, 103 - 24 * i) if side_of == 0 else (24 * i + 1, 25 + 24 * i)
                     from_edge = lane if side_of == 0 else 127 - lane
-                    packed[i, m] = jnp.where(
+                    a = i if side_of == 0 else 3 - i
+                    out_ref[pl.ds((m // 8) * 32 + m % 8 + 8 * a, 8, stride=64), :] = jnp.where(
                         from_edge < 115 - 24 * i,
                         pltpu.roll(both[i], (sh1 - m) % 128, axis=1), pltpu.roll(both[i + 1], (sh2 - m) % 128, axis=1),
                     )
@@ -401,15 +402,20 @@
     for copy in exchanges:
         copy.wait_recv()
     disp = [((mine[p] + got[0, p]) + (got[1, p] + got[2, p])) for p in range(4)]
-    back = dot3(jnp.concatenate(disp, axis=0), up_w[...])
-    for m in range(NM):
-        p = m // 4
-        local = NM * (sub & 3) + m
-        tissue = ((local + lax.shift_right_logical(k_own, 1)) & (ROWS - 1)) < k_own
-        for i in range(4):
-            a = jnp.where(tx == 0, i, 3 - i)
-            value = packed[i, m] + jnp.where(tissue, back[8 * p : 8 * p + 8, 128 * i : 128 * i + 128], 0.0)
-            out_ref[pl.ds((m // 8) * 32 + m % 8 + 8 * a, 8, stride=64), :] = value
+    back[...] = dot3(jnp.concatenate(disp, axis=0), up_w[...])
+    for r in range(ROWS // 8):
+        tissue = ((8 * r + sub + lax.shift_right_logical(k_own, 1)) & (ROWS - 1)) < k_own
+        for c in range(2):
+            first = 8 * (2 * r % 4) + 4 * c + r // 2
+            for i in range(4):
+                at = pl.ds((8 * c + r) * 32 + 8 * jnp.where(tx == 0, i, 3 - i), 8)
+                columns = pl.ds(128 * i, 128)
+                value = jnp.where(
+                    sub < 4,
+                    jnp.broadcast_to(back[pl.ds(first, 1), columns], (8, 128)),
+                    jnp.broadcast_to(back[pl.ds(first + 8, 1), columns], (8, 128)),
+                )
+                out_ref[at, :] = out_ref[at, :] + jnp.where(tissue, value, 0.0)
     for copy in exchanges:
         copy.wait_send()
 
@@ -434,7 +440,7 @@
             vmem((128, COLS), BF16),
             vmem((3, 4, 8, 128), F32),
             vmem((3, 4, 8, 128), F32),
-            vmem((4, NM, 8, 128), F32),
+            vmem((32, COLS), F32),
             pltpu.SMEM((32,), jnp.int32),
             pltpu.SemaphoreType.DMA((5,)),
             pltpu.SemaphoreType.DMA((11,)),

time: 20.1 us -> 20.1 us (level)
  no operation moved by 1% of the time
where the time goes in v7:
time: 20.1 us; the launch traced here: 19.9 us
  Pallas kernels  19.2 us (96%)
  local copies, waits for them, and re-layouts  0.71 us (4%)
    pallas_call x1, Pallas kernels, shards(): pl.pallas_call(kernel, out_shape=jax.ShapeDtypeStruct((2 * ROWS * 4, 128)...  19.2 us
    unnamed x1, local copies, waits for them, and re-layouts  0.71 us

profile of v7, /device:TPU:192, one launch (start us, length us, event | category | flops | bytes accessed | tf_op | source)
XLA Modules:
  0.0 19.9 jit_solution(2668725740284782887)
XLA Ops:
  0.0 19.2 %align.1 = f32[512,128]{1,0:T(8,128)S(1)} custom-call(s32[32]{0:T(128)} %tissue_hbm.1, f32[1,64,512]{2,1,0:T(8,128)} %img_ref.1), custom_call_target="tpu_custom_call" | custom-call | tf_op jit(solution)/shard_map/align/pallas_call | solution.py:425
  19.2 0.7 %copy.4 = f32[2,1,64,512]{3,2,1,0:T(8,128)} copy(f32[2,1,64,512]{3,2,1,0:T(8,128)S(1)} %bitcast.5) | data formatting | bytes 524288
